TPU v7x, 128 devices: a whole 4x4x4 slice. The times are simulated.
128 devices in a mesh: gz: 16 (over z_hi, x, core), xy: 8 (over z_lo, y).
Axes of the slice: x: 4, y: 4, z: 4 (z_hi: 2, z_lo: 2; z = z_hi * 2 + z_lo), core: 2. Of those that a mesh axis runs over, the one named last changes fastest.
Arguments:
- prior_estimate: float32 [768, 256, 128], P('gz', 'xy'), may hold values from 0.5 to 2
- views_upright: float32 [3, 768, 256, 128], P(None, 'gz', 'xy'), may hold values from 0.2 to 5
- views_turned: float32 [3, 768, 128, 256], P(None, 'gz', 'xy'), may hold values from 0.2 to 5
- kernel_depth: float32 [6, 61], replicated, may hold values from 0.005 to 1.55, as said below
- kernel_rows: float32 [6, 31], replicated, may hold values from 0.005 to 1.55, as said below
- kernel_columns: float32 [6, 31], replicated, may hold values from 0.005 to 1.55, as said below
- lateral_offsets: int32 [6], replicated, may hold values from -8 to 8, as said below
- block_views: int32 [128, 3], replicated, may hold values from 0 to 5, all different within a row
Outputs:
- estimate: float32 [768, 256, 128], P('gz', 'xy')
Inputs may be any that keep to these rules, and one draw needn't show every extreme that they name: `block_views`: row r holds 3 different views and belongs to the block at position r // 8 along gz and r % 8 along xy. `lateral_offsets`: one view has offset 8 and another -8. `kernel_depth`: positive taps. `kernel_rows`: positive taps. `kernel_columns`: positive taps.
All inputs are finite; a program needn't handle non-finite values.
Results may differ from a plain program's by a relative error of at most 0.00005.
Values sent between devices are 32-bit elements; how exact they have to be, the bound alone decides.
A program may use at most 128 MiB of HBM per device.

v0:
```python
import jax
import jax.numpy as jnp
from jax import lax
from jax.sharding import PartitionSpec as P

ITERS = 2


exact_mode = lax.Precision.HIGHEST


def padded(cells, sides, width):
    for axis, dim in sides:
        count = lax.axis_size(axis)
        ends = count - 1
        head = lax.slice_in_dim(cells, 0, width, axis=dim)
        tail = lax.slice_in_dim(cells, cells.shape[dim] - width, cells.shape[dim], axis=dim)
        cells = jnp.concatenate(
            [
                lax.ppermute(tail, axis, [(i, (i + 1) % count) for i in range(ends)]),
                cells,
                lax.ppermute(head, axis, [((i + 1) % count, i) for i in range(ends)]),
            ],
            axis=dim,
        )
    return cells


def band_matrix(kernel, length):
    extent = kernel.shape[0]
    row_index = jnp.arange(length, dtype=jnp.int32)[:, None]
    col_index = jnp.arange(length + extent - 1, dtype=jnp.int32)[None, :]
    offset = col_index - row_index
    choose = (offset[:, :, None] == jnp.arange(extent, dtype=jnp.int32)[None, None, :]).astype(
        jnp.float32
    )
    return jnp.sum(choose * kernel[None, None, :], axis=2)


def lateral_matrix(kernel, displacement, length):
    extent = kernel.shape[0]
    radius = (extent - 1) // 2
    row_index = jnp.arange(length, dtype=jnp.int32)[:, None]
    col_index = jnp.arange(length, dtype=jnp.int32)[None, :]
    offset = col_index - row_index + radius + displacement
    choose = (offset[:, :, None] == jnp.arange(extent, dtype=jnp.int32)[None, None, :]).astype(
        jnp.float32
    )
    return jnp.sum(choose * kernel[None, None, :], axis=2)


def normalize(kernel):
    return kernel / jnp.sum(kernel, axis=-1, keepdims=True)


def blur_forward(haloed, band_depth, band_rows, lateral):
    section = jnp.einsum("zj,jyx->zyx", band_depth, haloed, precision=exact_mode)
    section = jnp.einsum("yj,zjx->zyx", band_rows, section, precision=exact_mode)
    return jnp.einsum("zyj,xj->zyx", section, lateral, precision=exact_mode)


def local(
    prior_estimate,
    views_upright,
    views_turned,
    kernel_depth,
    kernel_rows,
    kernel_columns,
    lateral_offsets,
    block_views,
):
    depth, rows, columns = prior_estimate.shape
    count_views = kernel_depth.shape[0]
    count_blocks = block_views.shape[0]
    count_active = block_views.shape[1]
    reach_depth = (kernel_depth.shape[1] - 1) // 2
    reach_rows = (kernel_rows.shape[1] - 1) // 2
    turned = jnp.transpose(
        lax.all_to_all(views_turned, "xy", split_axis=3, concat_axis=2, tiled=True), (0, 1, 3, 2)
    )
    observed = jnp.concatenate([views_upright, turned], axis=0)
    taps_depth = normalize(kernel_depth)
    taps_rows = normalize(kernel_rows)
    taps_columns = normalize(kernel_columns)
    forward_depth = [band_matrix(taps_depth[number], depth) for number in range(count_views)]
    forward_rows = [band_matrix(taps_rows[number], rows) for number in range(count_views)]
    laterals = [
        lateral_matrix(taps_columns[number], lateral_offsets[number], columns)
        for number in range(count_views)
    ]
    member = (
        jnp.sum(
            (
                block_views[:, :, None] == jnp.arange(count_views, dtype=jnp.int32)[None, None, :]
            ).astype(jnp.float32),
            axis=1,
        )
        / count_active
    )
    side_count = lax.axis_size("xy")
    here_depth = lax.axis_index("gz")
    here_rows = lax.axis_index("xy")
    block_list = jnp.arange(count_blocks, dtype=jnp.int32)
    own_id = here_depth * side_count + here_rows
    picker = (block_list == own_id).astype(jnp.float32)
    own_weights = jnp.dot(picker, member, precision=exact_mode)
    adjoint_depth = [band_matrix(taps_depth[number][::-1], depth) for number in range(count_views)]
    adjoint_rows = [band_matrix(taps_rows[number][::-1], rows) for number in range(count_views)]
    estimate = prior_estimate
    for iteration in range(ITERS):
        haloed = padded(estimate, (("xy", 1),), reach_rows)
        haloed = padded(haloed, (("gz", 0),), reach_depth)
        correction = jnp.zeros_like(estimate)
        for number in range(count_views):
            blurred = blur_forward(
                haloed, forward_depth[number], forward_rows[number], laterals[number]
            )
            quotient = observed[number] / blurred
            rimmed = padded(quotient, (("xy", 1),), reach_rows)
            rimmed = padded(rimmed, (("gz", 0),), reach_depth)
            back = jnp.einsum("zj,jyx->zyx", adjoint_depth[number], rimmed, precision=exact_mode)
            back = jnp.einsum("yj,zjx->zyx", adjoint_rows[number], back, precision=exact_mode)
            back = jnp.einsum("zyj,jx->zyx", back, laterals[number], precision=exact_mode)
            correction = correction + own_weights[number] * back
        estimate = estimate * correction
    return estimate


def solution(mesh):
    in_specs = (
        P("gz", "xy", None),
        P(None, "gz", "xy", None),
        P(None, "gz", "xy", None),
        P(),
        P(),
        P(),
        P(),
        P(),
    )
    out_specs = P("gz", "xy", None)
    return jax.shard_map(local, mesh=mesh, in_specs=in_specs, out_specs=out_specs, check_vma=False)
```

profile of v0, /device:TPU:31, one launch (start us, length us, event | category | flops | bytes accessed | tf_op | source)
XLA Modules:
  0.0 543.5 jit_solution(17599730964510681161)
XLA Ops:
  7.6 5.5 %copy.134 = f32[3,48,16,256]{1,2,0,3:T(8,128)} copy(f32[3,48,16,256]{3,2,1,0:T(8,128)S(1)} %copy-done.8) | data formatting | bytes 4718592 | tf_op args[2]
  13.1 9.5 %reshape.154 = f32[8,1,73728]{2,1,0:T(1,128)} reshape(f32[256,3,16,48]{3,2,1,0:T(8,128)} %bitcast.336) | data formatting | bytes 4718592
  22.6 6.2 %all-to-all-start = ((f32[8,1,73728]{2,1,0:T(1,128)}), f32[8,1,73728]{2,1,0:T(1,128)S(1)}, u32[]{:S(2)}, u32[]{:S(2)}) async-start(f32[8,1,73728]{2,1,0:T(1,128)} %reshape.154), calls=%async_computation | async-start | bytes 4718592 | tf_op jit(solution)/shard_map/all_to_all | solution.py:79
  69.8 5.6 %collective-permute-start.2 = (f32[30,62,128]{2,1,0:T(8,128)S(1)}, f32[30,62,128]{2,1,0:T(8,128)S(1)}, u32[]{:S(2)}, u32[]{:S(2)}) collective-permute-start(f32[30,62,128]{2,1,0:T(8,128)S(1)} %copy.121), channel_id=1, source_target_pairs={{0,8},{8,16},{16,24},{24,32},{32,40},{40,48},{48,56},{56,64},{64,7... | collective-permute-start | bytes 2856968 | tf_op jit(solution)/shard_map/ppermute | solution.py:20
  124.8 5.5 %collective-permute-start.8 = (f32[48,15,128]{2,1,0:T(8,128)S(1)}, f32[48,15,128]{2,1,0:T(8,128)S(1)}, u32[]{:S(2)}, u32[]{:S(2)}) collective-permute-start(f32[48,15,128]{2,1,0:T(8,128)S(1)} %get-tuple-element.73), channel_id=1, source_target_pairs={{0,1},{1,2},{2,3},{3,4},{4,5},{5,6},{6,7},{8,9},{9,10},{10,11},{11... | collective-permute-start | bytes 1105928 | tf_op jit(solution)/shard_map/ppermute | solution.py:20
  139.2 8.2 %collective-permute-done.4 = f32[48,15,128]{2,1,0:T(8,128)S(1)} collective-permute-done((f32[48,15,128]{2,1,0:T(8,128)S(1)}, f32[48,15,128]{2,1,0:T(8,128)S(1)}, u32[]{:S(2)}, u32[]{:S(2)}) %collective-permute-start.4) | collective-permute-done | bytes 368672 | tf_op jit(solution)/shard_map/ppermute | solution.py:20
  152.3 8.7 %reduce = f32[8,73728]{1,0:T(8,128)} reduce(f32[8,1,73728]{2,1,0:T(1,128)S(1)} %all-to-all-done, f32[]{:T(128)} %broadcast.179), dimensions={1}, to_apply=%all_to_all.13.reduce_sub_computation | reduce | bytes 4718596 | tf_op jit(solution)/shard_map/all_to_all | solution.py:79
  161.1 6.8 %reshape.155 = f32[256,3,16,48]{3,2,1,0:T(8,128)} reshape(f32[8,73728]{1,0:T(8,128)} %reduce) | data formatting | bytes 4718592
  167.9 8.1 %copy.136 = f32[3,48,8,16,32]{1,4,3,2,0:T(8,128)} copy(f32[3,48,8,16,32]{1,3,0,4,2:T(8,128)} %bitcast.334) | data formatting | bytes 4718592 | tf_op jit(solution)/shard_map/all_to_all | solution.py:79
  175.9 5.9 %copy.137 = f32[3,48,128,32]{2,3,1,0:T(8,128)S(1)} copy(f32[3,48,128,32]{1,3,2,0:T(8,128)} %bitcast.335) | data formatting | bytes 4718592 | tf_op jit(solution)/shard_map/all_to_all | solution.py:79
  185.9 6.2 %collective-permute-start.24 = (f32[48,15,128]{2,1,0:T(8,128)S(1)}, f32[48,15,128]{2,1,0:T(8,128)S(1)}, u32[]{:S(2)}, u32[]{:S(2)}) collective-permute-start(f32[48,15,128]{2,1,0:T(8,128)S(1)} %get-tuple-element.81), channel_id=1, source_target_pairs={{0,1},{1,2},{2,3},{3,4},{4,5},{5,6},{6,7},{8,9},{9,10},{10,11},{11... | collective-permute-start | bytes 1105928 | tf_op jit(solution)/shard_map/ppermute | solution.py:20
  194.9 5.5 %collective-permute-start.20 = (f32[48,15,128]{2,1,0:T(8,128)S(1)}, f32[48,15,128]{2,1,0:T(8,128)S(1)}, u32[]{:S(2)}, u32[]{:S(2)}) collective-permute-start(f32[48,15,128]{2,1,0:T(8,128)S(1)} %get-tuple-element.79), channel_id=1, source_target_pairs={{0,1},{1,2},{2,3},{3,4},{4,5},{5,6},{6,7},{8,9},{9,10},{10,11},{11... | collective-permute-start | bytes 1105928 | tf_op jit(solution)/shard_map/ppermute | solution.py:20
  203.4 5.5 %collective-permute-start.16 = (f32[48,15,128]{2,1,0:T(8,128)S(1)}, f32[48,15,128]{2,1,0:T(8,128)S(1)}, u32[]{:S(2)}, u32[]{:S(2)}) collective-permute-start(f32[48,15,128]{2,1,0:T(8,128)S(1)} %get-tuple-element.77), channel_id=1, source_target_pairs={{0,1},{1,2},{2,3},{3,4},{4,5},{5,6},{6,7},{8,9},{9,10},{10,11},{11... | collective-permute-start | bytes 1105928 | tf_op jit(solution)/shard_map/ppermute | solution.py:20
  221.0 7.3 %collective-permute-start.10 = (f32[30,62,128]{2,1,0:T(8,128)S(1)}, f32[30,62,128]{2,1,0:T(8,128)S(1)}, u32[]{:S(2)}, u32[]{:S(2)}) collective-permute-start(f32[30,62,128]{2,1,0:T(8,128)S(1)} %copy-done.19), channel_id=1, source_target_pairs={{0,8},{8,16},{16,24},{24,32},{32,40},{40,48},{48,56},{56,64},{64,7... | collective-permute-start | bytes 2856968 | tf_op jit(solution)/shard_map/ppermute | solution.py:20
  231.1 7.4 %collective-permute-start.6 = (f32[30,62,128]{2,1,0:T(8,128)S(1)}, f32[30,62,128]{2,1,0:T(8,128)S(1)}, u32[]{:S(2)}, u32[]{:S(2)}) collective-permute-start(f32[30,62,128]{2,1,0:T(8,128)S(1)} %get-tuple-element.43), channel_id=1, source_target_pairs={{0,8},{8,16},{16,24},{24,32},{32,40},{40,48},{48,56},{56,64},{64,7... | collective-permute-start | bytes 2856968 | tf_op jit(solution)/shard_map/ppermute | solution.py:20
  247.0 7.3 %collective-permute-start.26 = (f32[30,62,128]{2,1,0:T(8,128)S(1)}, f32[30,62,128]{2,1,0:T(8,128)S(1)}, u32[]{:S(2)}, u32[]{:S(2)}) collective-permute-start(f32[30,62,128]{2,1,0:T(8,128)S(1)} %get-tuple-element.53), channel_id=1, source_target_pairs={{0,8},{8,16},{16,24},{24,32},{32,40},{40,48},{48,56},{56,64},{64,7... | collective-permute-start | bytes 2856968 | tf_op jit(solution)/shard_map/ppermute | solution.py:20
  264.4 7.3 %collective-permute-start.22 = (f32[30,62,128]{2,1,0:T(8,128)S(1)}, f32[30,62,128]{2,1,0:T(8,128)S(1)}, u32[]{:S(2)}, u32[]{:S(2)}) collective-permute-start(f32[30,62,128]{2,1,0:T(8,128)S(1)} %get-tuple-element.51), channel_id=1, source_target_pairs={{0,8},{8,16},{16,24},{24,32},{32,40},{40,48},{48,56},{56,64},{64,7... | collective-permute-start | bytes 2856968 | tf_op jit(solution)/shard_map/ppermute | solution.py:20
  281.6 7.5 %collective-permute-start.18 = (f32[30,62,128]{2,1,0:T(8,128)S(1)}, f32[30,62,128]{2,1,0:T(8,128)S(1)}, u32[]{:S(2)}, u32[]{:S(2)}) collective-permute-start(f32[30,62,128]{2,1,0:T(8,128)S(1)} %get-tuple-element.49), channel_id=1, source_target_pairs={{0,8},{8,16},{16,24},{24,32},{32,40},{40,48},{48,56},{56,64},{64,7... | collective-permute-start | bytes 2856968 | tf_op jit(solution)/shard_map/ppermute | solution.py:20
  316.1 5.5 %collective-permute-start.28 = (f32[48,15,128]{2,1,0:T(8,128)S(1)}, f32[48,15,128]{2,1,0:T(8,128)S(1)}, u32[]{:S(2)}, u32[]{:S(2)}) collective-permute-start(f32[48,15,128]{2,1,0:T(8,128)S(1)} %get-tuple-element.69), channel_id=1, source_target_pairs={{0,1},{1,2},{2,3},{3,4},{4,5},{5,6},{6,7},{8,9},{9,10},{10,11},{11... | collective-permute-start | bytes 1105928 | tf_op jit(solution)/shard_map/ppermute | solution.py:20
  328.7 7.4 %collective-permute-start.30 = (f32[30,62,128]{2,1,0:T(8,128)S(1)}, f32[30,62,128]{2,1,0:T(8,128)S(1)}, u32[]{:S(2)}, u32[]{:S(2)}) collective-permute-start(f32[30,62,128]{2,1,0:T(8,128)S(1)} %get-tuple-element.41), channel_id=1, source_target_pairs={{0,8},{8,16},{16,24},{24,32},{32,40},{40,48},{48,56},{56,64},{64,7... | collective-permute-start | bytes 2856968 | tf_op jit(solution)/shard_map/ppermute | solution.py:20
  336.1 9.7 %collective-permute-done.31 = f32[30,62,128]{2,1,0:T(8,128)S(1)} collective-permute-done((f32[30,62,128]{2,1,0:T(8,128)S(1)}, f32[30,62,128]{2,1,0:T(8,128)S(1)}, u32[]{:S(2)}, u32[]{:S(2)}) %collective-permute-start.31) | collective-permute-done | bytes 952352 | tf_op jit(solution)/shard_map/ppermute | solution.py:22
  376.7 5.9 %collective-permute-start.52 = (f32[48,15,128]{2,1,0:T(8,128)S(1)}, f32[48,15,128]{2,1,0:T(8,128)S(1)}, u32[]{:S(2)}, u32[]{:S(2)}) collective-permute-start(f32[48,15,128]{2,1,0:T(8,128)S(1)} %get-tuple-element.67), channel_id=1, source_target_pairs={{0,1},{1,2},{2,3},{3,4},{4,5},{5,6},{6,7},{8,9},{9,10},{10,11},{11... | collective-permute-start | bytes 1105928 | tf_op jit(solution)/shard_map/ppermute | solution.py:20
  386.9 5.5 %collective-permute-start.48 = (f32[48,15,128]{2,1,0:T(8,128)S(1)}, f32[48,15,128]{2,1,0:T(8,128)S(1)}, u32[]{:S(2)}, u32[]{:S(2)}) collective-permute-start(f32[48,15,128]{2,1,0:T(8,128)S(1)} %get-tuple-element.65), channel_id=1, source_target_pairs={{0,1},{1,2},{2,3},{3,4},{4,5},{5,6},{6,7},{8,9},{9,10},{10,11},{11... | collective-permute-start | bytes 1105928 | tf_op jit(solution)/shard_map/ppermute | solution.py:20
  404.3 5.5 %collective-permute-start.44 = (f32[48,15,128]{2,1,0:T(8,128)S(1)}, f32[48,15,128]{2,1,0:T(8,128)S(1)}, u32[]{:S(2)}, u32[]{:S(2)}) collective-permute-start(f32[48,15,128]{2,1,0:T(8,128)S(1)} %get-tuple-element.63), channel_id=1, source_target_pairs={{0,1},{1,2},{2,3},{3,4},{4,5},{5,6},{6,7},{8,9},{9,10},{10,11},{11... | collective-permute-start | bytes 1105928 | tf_op jit(solution)/shard_map/ppermute | solution.py:20
  412.0 5.5 %collective-permute-start.40 = (f32[48,15,128]{2,1,0:T(8,128)S(1)}, f32[48,15,128]{2,1,0:T(8,128)S(1)}, u32[]{:S(2)}, u32[]{:S(2)}) collective-permute-start(f32[48,15,128]{2,1,0:T(8,128)S(1)} %get-tuple-element.61), channel_id=1, source_target_pairs={{0,1},{1,2},{2,3},{3,4},{4,5},{5,6},{6,7},{8,9},{9,10},{10,11},{11... | collective-permute-start | bytes 1105928 | tf_op jit(solution)/shard_map/ppermute | solution.py:20
  427.5 5.5 %collective-permute-start.32 = (f32[48,15,128]{2,1,0:T(8,128)S(1)}, f32[48,15,128]{2,1,0:T(8,128)S(1)}, u32[]{:S(2)}, u32[]{:S(2)}) collective-permute-start(f32[48,15,128]{2,1,0:T(8,128)S(1)} %get-tuple-element.57), channel_id=1, source_target_pairs={{0,1},{1,2},{2,3},{3,4},{4,5},{5,6},{6,7},{8,9},{9,10},{10,11},{11... | collective-permute-start | bytes 1105928 | tf_op jit(solution)/shard_map/ppermute | solution.py:20
  435.4 11.7 %collective-permute-start.54 = (f32[30,62,128]{2,1,0:T(8,128)S(1)}, f32[30,62,128]{2,1,0:T(8,128)S(1)}, u32[]{:S(2)}, u32[]{:S(2)}) collective-permute-start(f32[30,62,128]{2,1,0:T(8,128)S(1)} %get-tuple-element.39), channel_id=1, source_target_pairs={{0,8},{8,16},{16,24},{24,32},{32,40},{40,48},{48,56},{56,64},{64,7... | collective-permute-start | bytes 2856968 | tf_op jit(solution)/shard_map/ppermute | solution.py:20
  449.5 7.3 %collective-permute-start.50 = (f32[30,62,128]{2,1,0:T(8,128)S(1)}, f32[30,62,128]{2,1,0:T(8,128)S(1)}, u32[]{:S(2)}, u32[]{:S(2)}) collective-permute-start(f32[30,62,128]{2,1,0:T(8,128)S(1)} %get-tuple-element.37), channel_id=1, source_target_pairs={{0,8},{8,16},{16,24},{24,32},{32,40},{40,48},{48,56},{56,64},{64,7... | collective-permute-start | bytes 2856968 | tf_op jit(solution)/shard_map/ppermute | solution.py:20
  459.5 7.3 %collective-permute-start.46 = (f32[30,62,128]{2,1,0:T(8,128)S(1)}, f32[30,62,128]{2,1,0:T(8,128)S(1)}, u32[]{:S(2)}, u32[]{:S(2)}) collective-permute-start(f32[30,62,128]{2,1,0:T(8,128)S(1)} %get-tuple-element.35), channel_id=1, source_target_pairs={{0,8},{8,16},{16,24},{24,32},{32,40},{40,48},{48,56},{56,64},{64,7... | collective-permute-start | bytes 2856968 | tf_op jit(solution)/shard_map/ppermute | solution.py:20
  477.3 7.3 %collective-permute-start.42 = (f32[30,62,128]{2,1,0:T(8,128)S(1)}, f32[30,62,128]{2,1,0:T(8,128)S(1)}, u32[]{:S(2)}, u32[]{:S(2)}) collective-permute-start(f32[30,62,128]{2,1,0:T(8,128)S(1)} %get-tuple-element.33), channel_id=1, source_target_pairs={{0,8},{8,16},{16,24},{24,32},{32,40},{40,48},{48,56},{56,64},{64,7... | collective-permute-start | bytes 2856968 | tf_op jit(solution)/shard_map/ppermute | solution.py:20
  494.4 7.3 %collective-permute-start.38 = (f32[30,62,128]{2,1,0:T(8,128)S(1)}, f32[30,62,128]{2,1,0:T(8,128)S(1)}, u32[]{:S(2)}, u32[]{:S(2)}) collective-permute-start(f32[30,62,128]{2,1,0:T(8,128)S(1)} %get-tuple-element.31), channel_id=1, source_target_pairs={{0,8},{8,16},{16,24},{24,32},{32,40},{40,48},{48,56},{56,64},{64,7... | collective-permute-start | bytes 2856968 | tf_op jit(solution)/shard_map/ppermute | solution.py:20
  511.6 7.4 %collective-permute-start.34 = (f32[30,62,128]{2,1,0:T(8,128)S(1)}, f32[30,62,128]{2,1,0:T(8,128)S(1)}, u32[]{:S(2)}, u32[]{:S(2)}) collective-permute-start(f32[30,62,128]{2,1,0:T(8,128)S(1)} %get-tuple-element.29), channel_id=1, source_target_pairs={{0,8},{8,16},{16,24},{24,32},{32,40},{40,48},{48,56},{56,64},{64,7... | collective-permute-start | bytes 2856968 | tf_op jit(solution)/shard_map/ppermute | solution.py:20
  (502 shorter events, 317.7 us)
Async XLA Ops:
  2.2 59.6 %collective-permute-start = (f32[48,15,128]{2,0,1:T(8,128)}, f32[48,15,128]{2,0,1:T(8,128)}, u32[]{:S(2)}, u32[]{:S(2)}) collective-permute-start(f32[48,15,128]{2,0,1:T(8,128)} %copy.306), channel_id=1, source_target_pairs={{0,1},{1,2},{2,3},{3,4},{4,5},{5,6},{6,7},{8,9},{9,10},{10,11},{11... | collective-permute-start | bytes 1105928 | tf_op jit(solution)/shard_map/ppermute | solution.py:20
  5.5 57.8 %collective-permute-start.1 = (f32[48,15,128]{2,0,1:T(8,128)S(1)}, f32[48,15,128]{2,0,1:T(8,128)}, u32[]{:S(2)}, u32[]{:S(2)}) collective-permute-start(f32[48,15,128]{2,0,1:T(8,128)S(1)} %copy.307), channel_id=1, source_target_pairs={{1,0},{2,1},{3,2},{4,3},{5,4},{6,5},{7,6},{9,8},{10,9},{11,10},{12... | collective-permute-start | bytes 1105928 | tf_op jit(solution)/shard_map/ppermute | solution.py:22
  22.6 129.2 %all-to-all-start = ((f32[8,1,73728]{2,1,0:T(1,128)}), f32[8,1,73728]{2,1,0:T(1,128)S(1)}, u32[]{:S(2)}, u32[]{:S(2)}) async-start(f32[8,1,73728]{2,1,0:T(1,128)} %reshape.154), calls=%async_computation | async-start | bytes 4718592 | tf_op jit(solution)/shard_map/all_to_all | solution.py:79
  94.0 36.3 %collective-permute-start.13 = (f32[48,15,128]{2,1,0:T(8,128)S(1)}, f32[48,15,128]{2,1,0:T(8,128)S(1)}, u32[]{:S(2)}, u32[]{:S(2)}) collective-permute-start(f32[48,15,128]{2,1,0:T(8,128)S(1)} %get-tuple-element.76), channel_id=1, source_target_pairs={{1,0},{2,1},{3,2},{4,3},{5,4},{6,5},{7,6},{9,8},{10,9},{11,10},{12... | collective-permute-start | bytes 1105928 | tf_op jit(solution)/shard_map/ppermute | solution.py:22
  96.5 39.8 %collective-permute-start.12 = (f32[48,15,128]{2,1,0:T(8,128)S(1)}, f32[48,15,128]{2,1,0:T(8,128)S(1)}, u32[]{:S(2)}, u32[]{:S(2)}) collective-permute-start(f32[48,15,128]{2,1,0:T(8,128)S(1)} %get-tuple-element.75), channel_id=1, source_target_pairs={{0,1},{1,2},{2,3},{3,4},{4,5},{5,6},{6,7},{8,9},{9,10},{10,11},{11... | collective-permute-start | bytes 1105928 | tf_op jit(solution)/shard_map/ppermute | solution.py:20
  106.3 30.1 %collective-permute-start.9 = (f32[48,15,128]{2,1,0:T(8,128)S(1)}, f32[48,15,128]{2,1,0:T(8,128)S(1)}, u32[]{:S(2)}, u32[]{:S(2)}) collective-permute-start(f32[48,15,128]{2,1,0:T(8,128)S(1)} %get-tuple-element.74), channel_id=1, source_target_pairs={{1,0},{2,1},{3,2},{4,3},{5,4},{6,5},{7,6},{9,8},{10,9},{11,10},{12... | collective-permute-start | bytes 1105928 | tf_op jit(solution)/shard_map/ppermute | solution.py:22
  218.9 28.1 %collective-permute-start.11 = (f32[30,62,128]{2,1,0:T(8,128)S(1)}, f32[30,62,128]{2,1,0:T(8,128)S(1)}, u32[]{:S(2)}, u32[]{:S(2)}) collective-permute-start(f32[30,62,128]{2,1,0:T(8,128)S(1)} %copy-done.20), channel_id=1, source_target_pairs={{8,0},{16,8},{24,16},{32,24},{40,32},{48,40},{56,48},{64,56},{72,6... | collective-permute-start | bytes 2856968 | tf_op jit(solution)/shard_map/ppermute | solution.py:22
  221.0 33.2 %collective-permute-start.10 = (f32[30,62,128]{2,1,0:T(8,128)S(1)}, f32[30,62,128]{2,1,0:T(8,128)S(1)}, u32[]{:S(2)}, u32[]{:S(2)}) collective-permute-start(f32[30,62,128]{2,1,0:T(8,128)S(1)} %copy-done.19), channel_id=1, source_target_pairs={{0,8},{8,16},{16,24},{24,32},{32,40},{40,48},{48,56},{56,64},{64,7... | collective-permute-start | bytes 2856968 | tf_op jit(solution)/shard_map/ppermute | solution.py:20
  228.3 36.1 %collective-permute-start.7 = (f32[30,62,128]{2,1,0:T(8,128)S(1)}, f32[30,62,128]{2,1,0:T(8,128)S(1)}, u32[]{:S(2)}, u32[]{:S(2)}) collective-permute-start(f32[30,62,128]{2,1,0:T(8,128)S(1)} %get-tuple-element.44), channel_id=1, source_target_pairs={{8,0},{16,8},{24,16},{32,24},{40,32},{48,40},{56,48},{64,56},{72,6... | collective-permute-start | bytes 2856968 | tf_op jit(solution)/shard_map/ppermute | solution.py:22
  231.1 40.5 %collective-permute-start.6 = (f32[30,62,128]{2,1,0:T(8,128)S(1)}, f32[30,62,128]{2,1,0:T(8,128)S(1)}, u32[]{:S(2)}, u32[]{:S(2)}) collective-permute-start(f32[30,62,128]{2,1,0:T(8,128)S(1)} %get-tuple-element.43), channel_id=1, source_target_pairs={{0,8},{8,16},{16,24},{24,32},{32,40},{40,48},{48,56},{56,64},{64,7... | collective-permute-start | bytes 2856968 | tf_op jit(solution)/shard_map/ppermute | solution.py:20
  238.6 43.0 %collective-permute-start.27 = (f32[30,62,128]{2,1,0:T(8,128)S(1)}, f32[30,62,128]{2,1,0:T(8,128)S(1)}, u32[]{:S(2)}, u32[]{:S(2)}) collective-permute-start(f32[30,62,128]{2,1,0:T(8,128)S(1)} %get-tuple-element.54), channel_id=1, source_target_pairs={{8,0},{16,8},{24,16},{32,24},{40,32},{48,40},{56,48},{64,56},{72,6... | collective-permute-start | bytes 2856968 | tf_op jit(solution)/shard_map/ppermute | solution.py:22
  247.0 42.1 %collective-permute-start.26 = (f32[30,62,128]{2,1,0:T(8,128)S(1)}, f32[30,62,128]{2,1,0:T(8,128)S(1)}, u32[]{:S(2)}, u32[]{:S(2)}) collective-permute-start(f32[30,62,128]{2,1,0:T(8,128)S(1)} %get-tuple-element.53), channel_id=1, source_target_pairs={{0,8},{8,16},{16,24},{24,32},{32,40},{40,48},{48,56},{56,64},{64,7... | collective-permute-start | bytes 2856968 | tf_op jit(solution)/shard_map/ppermute | solution.py:20
  254.3 42.5 %collective-permute-start.23 = (f32[30,62,128]{2,1,0:T(8,128)S(1)}, f32[30,62,128]{2,1,0:T(8,128)S(1)}, u32[]{:S(2)}, u32[]{:S(2)}) collective-permute-start(f32[30,62,128]{2,1,0:T(8,128)S(1)} %get-tuple-element.52), channel_id=1, source_target_pairs={{8,0},{16,8},{24,16},{32,24},{40,32},{48,40},{56,48},{64,56},{72,6... | collective-permute-start | bytes 2856968 | tf_op jit(solution)/shard_map/ppermute | solution.py:22
  264.4 32.3 %collective-permute-start.22 = (f32[30,62,128]{2,1,0:T(8,128)S(1)}, f32[30,62,128]{2,1,0:T(8,128)S(1)}, u32[]{:S(2)}, u32[]{:S(2)}) collective-permute-start(f32[30,62,128]{2,1,0:T(8,128)S(1)} %get-tuple-element.51), channel_id=1, source_target_pairs={{0,8},{8,16},{16,24},{24,32},{32,40},{40,48},{48,56},{56,64},{64,7... | collective-permute-start | bytes 2856968 | tf_op jit(solution)/shard_map/ppermute | solution.py:20
  271.7 33.1 %collective-permute-start.19 = (f32[30,62,128]{2,1,0:T(8,128)S(1)}, f32[30,62,128]{2,1,0:T(8,128)S(1)}, u32[]{:S(2)}, u32[]{:S(2)}) collective-permute-start(f32[30,62,128]{2,1,0:T(8,128)S(1)} %get-tuple-element.50), channel_id=1, source_target_pairs={{8,0},{16,8},{24,16},{32,24},{40,32},{48,40},{56,48},{64,56},{72,6... | collective-permute-start | bytes 2856968 | tf_op jit(solution)/shard_map/ppermute | solution.py:22
  374.7 29.6 %collective-permute-start.53 = (f32[48,15,128]{2,1,0:T(8,128)S(1)}, f32[48,15,128]{2,1,0:T(8,128)S(1)}, u32[]{:S(2)}, u32[]{:S(2)}) collective-permute-start(f32[48,15,128]{2,1,0:T(8,128)S(1)} %get-tuple-element.68), channel_id=1, source_target_pairs={{1,0},{2,1},{3,2},{4,3},{5,4},{6,5},{7,6},{9,8},{10,9},{11,10},{12... | collective-permute-start | bytes 1105928 | tf_op jit(solution)/shard_map/ppermute | solution.py:22
  376.7 33.2 %collective-permute-start.52 = (f32[48,15,128]{2,1,0:T(8,128)S(1)}, f32[48,15,128]{2,1,0:T(8,128)S(1)}, u32[]{:S(2)}, u32[]{:S(2)}) collective-permute-start(f32[48,15,128]{2,1,0:T(8,128)S(1)} %get-tuple-element.67), channel_id=1, source_target_pairs={{0,1},{1,2},{2,3},{3,4},{4,5},{5,6},{6,7},{8,9},{9,10},{10,11},{11... | collective-permute-start | bytes 1105928 | tf_op jit(solution)/shard_map/ppermute | solution.py:20
  385.0 27.0 %collective-permute-start.49 = (f32[48,15,128]{2,1,0:T(8,128)S(1)}, f32[48,15,128]{2,1,0:T(8,128)S(1)}, u32[]{:S(2)}, u32[]{:S(2)}) collective-permute-start(f32[48,15,128]{2,1,0:T(8,128)S(1)} %get-tuple-element.66), channel_id=1, source_target_pairs={{1,0},{2,1},{3,2},{4,3},{5,4},{6,5},{7,6},{9,8},{10,9},{11,10},{12... | collective-permute-start | bytes 1105928 | tf_op jit(solution)/shard_map/ppermute | solution.py:22
  386.9 30.6 %collective-permute-start.48 = (f32[48,15,128]{2,1,0:T(8,128)S(1)}, f32[48,15,128]{2,1,0:T(8,128)S(1)}, u32[]{:S(2)}, u32[]{:S(2)}) collective-permute-start(f32[48,15,128]{2,1,0:T(8,128)S(1)} %get-tuple-element.65), channel_id=1, source_target_pairs={{0,1},{1,2},{2,3},{3,4},{4,5},{5,6},{6,7},{8,9},{9,10},{10,11},{11... | collective-permute-start | bytes 1105928 | tf_op jit(solution)/shard_map/ppermute | solution.py:20
  419.7 27.4 %collective-permute-start.36 = (f32[48,15,128]{2,1,0:T(8,128)S(1)}, f32[48,15,128]{2,1,0:T(8,128)S(1)}, u32[]{:S(2)}, u32[]{:S(2)}) collective-permute-start(f32[48,15,128]{2,1,0:T(8,128)S(1)} %get-tuple-element.59), channel_id=1, source_target_pairs={{0,1},{1,2},{2,3},{3,4},{4,5},{5,6},{6,7},{8,9},{9,10},{10,11},{11... | collective-permute-start | bytes 1105928 | tf_op jit(solution)/shard_map/ppermute | solution.py:20
  427.5 29.2 %collective-permute-start.32 = (f32[48,15,128]{2,1,0:T(8,128)S(1)}, f32[48,15,128]{2,1,0:T(8,128)S(1)}, u32[]{:S(2)}, u32[]{:S(2)}) collective-permute-start(f32[48,15,128]{2,1,0:T(8,128)S(1)} %get-tuple-element.57), channel_id=1, source_target_pairs={{0,1},{1,2},{2,3},{3,4},{4,5},{5,6},{6,7},{8,9},{9,10},{10,11},{11... | collective-permute-start | bytes 1105928 | tf_op jit(solution)/shard_map/ppermute | solution.py:20
  433.0 26.5 %collective-permute-start.55 = (f32[30,62,128]{2,1,0:T(8,128)S(1)}, f32[30,62,128]{2,1,0:T(8,128)S(1)}, u32[]{:S(2)}, u32[]{:S(2)}) collective-permute-start(f32[30,62,128]{2,1,0:T(8,128)S(1)} %get-tuple-element.40), channel_id=1, source_target_pairs={{8,0},{16,8},{24,16},{32,24},{40,32},{48,40},{56,48},{64,56},{72,6... | collective-permute-start | bytes 2856968 | tf_op jit(solution)/shard_map/ppermute | solution.py:22
  435.4 31.4 %collective-permute-start.54 = (f32[30,62,128]{2,1,0:T(8,128)S(1)}, f32[30,62,128]{2,1,0:T(8,128)S(1)}, u32[]{:S(2)}, u32[]{:S(2)}) collective-permute-start(f32[30,62,128]{2,1,0:T(8,128)S(1)} %get-tuple-element.39), channel_id=1, source_target_pairs={{0,8},{8,16},{16,24},{24,32},{32,40},{40,48},{48,56},{56,64},{64,7... | collective-permute-start | bytes 2856968 | tf_op jit(solution)/shard_map/ppermute | solution.py:20
  447.1 30.2 %collective-permute-start.51 = (f32[30,62,128]{2,1,0:T(8,128)S(1)}, f32[30,62,128]{2,1,0:T(8,128)S(1)}, u32[]{:S(2)}, u32[]{:S(2)}) collective-permute-start(f32[30,62,128]{2,1,0:T(8,128)S(1)} %get-tuple-element.38), channel_id=1, source_target_pairs={{8,0},{16,8},{24,16},{32,24},{40,32},{48,40},{56,48},{64,56},{72,6... | collective-permute-start | bytes 2856968 | tf_op jit(solution)/shard_map/ppermute | solution.py:22
  449.5 35.2 %collective-permute-start.50 = (f32[30,62,128]{2,1,0:T(8,128)S(1)}, f32[30,62,128]{2,1,0:T(8,128)S(1)}, u32[]{:S(2)}, u32[]{:S(2)}) collective-permute-start(f32[30,62,128]{2,1,0:T(8,128)S(1)} %get-tuple-element.37), channel_id=1, source_target_pairs={{0,8},{8,16},{16,24},{24,32},{32,40},{40,48},{48,56},{56,64},{64,7... | collective-permute-start | bytes 2856968 | tf_op jit(solution)/shard_map/ppermute | solution.py:20
  456.7 37.6 %collective-permute-start.47 = (f32[30,62,128]{2,1,0:T(8,128)S(1)}, f32[30,62,128]{2,1,0:T(8,128)S(1)}, u32[]{:S(2)}, u32[]{:S(2)}) collective-permute-start(f32[30,62,128]{2,1,0:T(8,128)S(1)} %get-tuple-element.36), channel_id=1, source_target_pairs={{8,0},{16,8},{24,16},{32,24},{40,32},{48,40},{56,48},{64,56},{72,6... | collective-permute-start | bytes 2856968 | tf_op jit(solution)/shard_map/ppermute | solution.py:22
  459.5 42.1 %collective-permute-start.46 = (f32[30,62,128]{2,1,0:T(8,128)S(1)}, f32[30,62,128]{2,1,0:T(8,128)S(1)}, u32[]{:S(2)}, u32[]{:S(2)}) collective-permute-start(f32[30,62,128]{2,1,0:T(8,128)S(1)} %get-tuple-element.35), channel_id=1, source_target_pairs={{0,8},{8,16},{16,24},{24,32},{32,40},{40,48},{48,56},{56,64},{64,7... | collective-permute-start | bytes 2856968 | tf_op jit(solution)/shard_map/ppermute | solution.py:20
  466.8 44.7 %collective-permute-start.43 = (f32[30,62,128]{2,1,0:T(8,128)S(1)}, f32[30,62,128]{2,1,0:T(8,128)S(1)}, u32[]{:S(2)}, u32[]{:S(2)}) collective-permute-start(f32[30,62,128]{2,1,0:T(8,128)S(1)} %get-tuple-element.34), channel_id=1, source_target_pairs={{8,0},{16,8},{24,16},{32,24},{40,32},{48,40},{56,48},{64,56},{72,6... | collective-permute-start | bytes 2856968 | tf_op jit(solution)/shard_map/ppermute | solution.py:22
  477.3 41.7 %collective-permute-start.42 = (f32[30,62,128]{2,1,0:T(8,128)S(1)}, f32[30,62,128]{2,1,0:T(8,128)S(1)}, u32[]{:S(2)}, u32[]{:S(2)}) collective-permute-start(f32[30,62,128]{2,1,0:T(8,128)S(1)} %get-tuple-element.33), channel_id=1, source_target_pairs={{0,8},{8,16},{16,24},{24,32},{32,40},{40,48},{48,56},{56,64},{64,7... | collective-permute-start | bytes 2856968 | tf_op jit(solution)/shard_map/ppermute | solution.py:20
  484.6 42.0 %collective-permute-start.39 = (f32[30,62,128]{2,1,0:T(8,128)S(1)}, f32[30,62,128]{2,1,0:T(8,128)S(1)}, u32[]{:S(2)}, u32[]{:S(2)}) collective-permute-start(f32[30,62,128]{2,1,0:T(8,128)S(1)} %get-tuple-element.32), channel_id=1, source_target_pairs={{8,0},{16,8},{24,16},{32,24},{40,32},{48,40},{56,48},{64,56},{72,6... | collective-permute-start | bytes 2856968 | tf_op jit(solution)/shard_map/ppermute | solution.py:22
  494.4 32.2 %collective-permute-start.38 = (f32[30,62,128]{2,1,0:T(8,128)S(1)}, f32[30,62,128]{2,1,0:T(8,128)S(1)}, u32[]{:S(2)}, u32[]{:S(2)}) collective-permute-start(f32[30,62,128]{2,1,0:T(8,128)S(1)} %get-tuple-element.31), channel_id=1, source_target_pairs={{0,8},{8,16},{16,24},{24,32},{32,40},{40,48},{48,56},{56,64},{64,7... | collective-permute-start | bytes 2856968 | tf_op jit(solution)/shard_map/ppermute | solution.py:20
  501.7 32.9 %collective-permute-start.35 = (f32[30,62,128]{2,1,0:T(8,128)S(1)}, f32[30,62,128]{2,1,0:T(8,128)S(1)}, u32[]{:S(2)}, u32[]{:S(2)}) collective-permute-start(f32[30,62,128]{2,1,0:T(8,128)S(1)} %get-tuple-element.30), channel_id=1, source_target_pairs={{8,0},{16,8},{24,16},{32,24},{40,32},{48,40},{56,48},{64,56},{72,6... | collective-permute-start | bytes 2856968 | tf_op jit(solution)/shard_map/ppermute | solution.py:22
  (145 other events, 2070.2 us)
where the time goes:
time: 552 us; the launch traced here: 544 us
  starting transfers between devices  244 us (44%)
  matrix products  156 us (28%)
  local copies, waits for them, and re-layouts  68.4 us (12%)
  other arithmetic  41.3 us (7%)
  waiting for transfers between devices  30.5 us (6%)
    ppermute x28, starting transfers between devices, padded(): lax.ppermute(tail, axis, [(i, (i + 1) % count) for i in range(ends)])  176 us
    ppermute x28, starting transfers between devices, padded(): lax.ppermute(head, axis, [((i + 1) % count, i) for i in range(ends)])  61.3 us
    dot_general x12, matrix products, local(): jnp.einsum('zj,jyx->zyx', adjoint_depth[number], rimmed, precision=exact_...  48.6 us
    dot_general x12, matrix products, blur_forward(): jnp.einsum('zj,jyx->zyx', band_depth, haloed, precision=exact_mode)  37.9 us
    unnamed x247, local copies, waits for them, and re-layouts  25.3 us
    dot_general x12, matrix products, blur_forward(): jnp.einsum('yj,zjx->zyx', band_rows, section, precision=exact_mode)  21.3 us
    dot_general x12, matrix products, local(): jnp.einsum('yj,zjx->zyx', adjoint_rows[number], back, precision=exact_mode)  18.9 us
    dot_general x12, matrix products, local(): jnp.einsum('zyj,jx->zyx', back, laterals[number], precision=exact_mode)  18.1 us
  transfers between devices with their start and end apart: 57, of which 8 were waited for; matrix products, arithmetic and copies ran while one was open for 34% of the time, Pallas kernels for 0%

commit v1 on v0

v1 whole, which is shorter than its diff:
```python
import functools

import jax
import jax.numpy as jnp
from jax import lax
from jax.experimental import pallas as pl
from jax.experimental.pallas import tpu as pltpu
from jax.sharding import PartitionSpec as P

ITERS = 2
F32 = jnp.float32
BF16 = jnp.bfloat16
MESH = pl.DeviceIdType.MESH


def split(value):
    high = value.astype(BF16)
    low = (value - high.astype(F32)).astype(BF16)
    return high, low


def banded(taps_ref, view, index, extent):
    total = lax.fori_loop(0, extent, lambda k, s: s + taps_ref[view, k], jnp.float32(0.0))

    def one(k, mat):
        return jnp.where(index == k, taps_ref[view, k], mat)

    mat = lax.fori_loop(0, extent, one, jnp.zeros(index.shape, F32))
    return mat / jnp.full(index.shape, total, F32)


def kernel(
    nz, ny, views, halfv, n_gz, n_xy, hz, hy, hx,
    kd_ref, kr_ref, kc_ref, off_ref, bv_ref, est_hbm, up_hbm, vt_hbm,
    out_ref,
    ext, mid, cor, rz, ry, obs, vt, pack, recv,
    zl, zf, stack, zt, yf, ya, xf, xa,
    load_sem, fz_send, fz_recv, fy_send, fy_recv, fc_send, fc_recv,
    az_send, az_recv, ac_send, ac_recv, ay_send, ay_recv, t_send, t_recv,
):
    g = lax.axis_index("gz")
    r = lax.axis_index("xy")
    rz_n = (hz - 1) // 2
    top = rz_n + nz
    cols = ny // 2
    has = {"zu": g < n_gz - 1, "zd": g > 0, "yu": r < n_xy - 1, "yd": r > 0}
    opposite = {"zu": "zd", "zd": "zu", "yu": "yd", "yd": "yu"}
    target = {"zu": {"gz": g + 1}, "zd": {"gz": g - 1}, "yu": {"xy": r + 1}, "yd": {"xy": r - 1}}

    loads = [
        pltpu.make_async_copy(est_hbm, ext.at[pl.ds(rz_n, nz), pl.ds(16, ny), :], load_sem.at[0]),
        pltpu.make_async_copy(vt_hbm, vt, load_sem.at[1]),
        pltpu.make_async_copy(up_hbm, obs.at[pl.ds(0, halfv)], load_sem.at[2]),
    ]
    for load in loads:
        load.start()

    barrier = pltpu.get_barrier_semaphore()
    for d in range(1, n_xy):
        pl.semaphore_signal(
            barrier, inc=1, device_id={"xy": lax.rem(r + d, n_xy)}, device_id_type=MESH
        )
    for way in ("zu", "zd"):
        @pl.when(has[way])
        def _():
            pl.semaphore_signal(barrier, inc=1, device_id=target[way], device_id_type=MESH)

    ext[pl.ds(top + rz_n, ext.shape[0] - top - rz_n)] = jnp.zeros(
        (ext.shape[0] - top - rz_n,) + ext.shape[1:], F32
    )

    @pl.when(jnp.logical_not(has["zd"]))
    def _():
        @pl.loop(0, rz_n)
        def _(i):
            ext[i] = jnp.zeros(ext.shape[1:], F32)

    @pl.when(jnp.logical_not(has["zu"]))
    def _():
        @pl.loop(top, top + rz_n)
        def _(i):
            ext[i] = jnp.zeros(ext.shape[1:], F32)

    @pl.when(jnp.logical_not(has["yd"]))
    def _():
        @pl.loop(rz_n, top)
        def _(i):
            ext[i, pl.ds(0, 16), :] = jnp.zeros((16, 128), F32)

    @pl.when(jnp.logical_not(has["yu"]))
    def _():
        @pl.loop(rz_n, top)
        def _(i):
            ext[i, pl.ds(16 + ny, 16), :] = jnp.zeros((16, 128), F32)

    def flow(way, src, dst, send, recv_sem, number):
        def make():
            return pltpu.make_async_remote_copy(
                src_ref=src, dst_ref=dst, send_sem=send.at[number], recv_sem=recv_sem.at[number],
                device_id=target[way], device_id_type=MESH,
            )

        def start():
            @pl.when(has[way])
            def _():
                make().start()

        def arrived():
            @pl.when(has[opposite[way]])
            def _():
                make().wait_recv()

        def sent():
            @pl.when(has[way])
            def _():
                make().wait_send()

        return start, arrived, sent

    def cut(ref, z0, count, y0, width):
        return ref.at[pl.ds(z0, count), pl.ds(y0, width), :]

    low_src, high_src = rz_n, top - rz_n
    fz = [
        flow("zu", cut(ext, high_src, rz_n, 16, ny), cut(ext, 0, rz_n, 16, ny), fz_send, fz_recv, 0),
        flow("zd", cut(ext, low_src, rz_n, 16, ny), cut(ext, top, rz_n, 16, ny), fz_send, fz_recv, 1),
    ]
    fy = [
        flow("yu", cut(ext, rz_n, nz, ny, 16), cut(ext, rz_n, nz, 0, 16), fy_send, fy_recv, 0),
        flow("yd", cut(ext, rz_n, nz, 16, 16), cut(ext, rz_n, nz, 16 + ny, 16), fy_send, fy_recv, 1),
    ]
    fc = []
    for n, y0 in enumerate((0, 16 + ny)):
        fc.append(flow("zu", cut(ext, high_src, rz_n, y0, 16), cut(ext, 0, rz_n, y0, 16), fc_send, fc_recv, 2 * n))
        fc.append(flow("zd", cut(ext, low_src, rz_n, y0, 16), cut(ext, top, rz_n, y0, 16), fc_send, fc_recv, 2 * n + 1))
    ac = []
    for n, y0 in enumerate((0, 16 + ny)):
        ac.append(flow("zu", cut(cor, top, rz_n, y0, 16), cut(rz.at[0], 0, rz_n, y0, 16), ac_send, ac_recv, 2 * n))
        ac.append(flow("zd", cut(cor, 0, rz_n, y0, 16), cut(rz.at[1], 0, rz_n, y0, 16), ac_send, ac_recv, 2 * n + 1))
    az = [
        flow("zu", cut(cor, top, rz_n, 16, ny), cut(rz.at[0], 0, rz_n, 16, ny), az_send, az_recv, 0),
        flow("zd", cut(cor, 0, rz_n, 16, ny), cut(rz.at[1], 0, rz_n, 16, ny), az_send, az_recv, 1),
    ]
    ay = [
        flow("yu", cut(cor, rz_n, nz, 16 + ny, 16), ry.at[0], ay_send, ay_recv, 0),
        flow("yd", cut(cor, rz_n, nz, 0, 16), ry.at[1], ay_send, ay_recv, 1),
    ]

    def begin(flows):
        for f in flows:
            f[0]()

    def await_all(flows):
        for f in flows:
            f[1]()

    def drain(flows):
        for f in flows:
            f[2]()

    loads[0].wait()
    greeted = n_xy - 1 + has["zu"].astype(jnp.int32) + has["zd"].astype(jnp.int32)
    pl.semaphore_wait(barrier, greeted)
    begin(fy)
    begin(fz)

    loads[1].wait()
    octets = nz // 8

    @pl.loop(0, halfv * octets)
    def _(i):
        view = i // octets
        octet = i % octets
        block = vt[view, pl.ds(octet * 8, 8)].reshape(128, ny * n_xy)
        for half in range(2):
            part = block[:, half * 128:(half + 1) * 128].T
            for piece in range(128 // ny):
                pack[half * (128 // ny) + piece, i] = part[piece * ny:(piece + 1) * ny]

    def turn(d):
        peer = lax.rem(r + d, n_xy)
        return pltpu.make_async_remote_copy(
            src_ref=pack.at[peer], dst_ref=recv.at[r], send_sem=t_send.at[d - 1], recv_sem=t_recv.at[d - 1],
            device_id={"xy": peer}, device_id_type=MESH,
        )

    for d in range(1, n_xy):
        turn(d).start()

    @pl.loop(0, halfv * octets)
    def _(i):
        recv[r, i] = pack[r, i]

    row = lambda shape: lax.broadcasted_iota(jnp.int32, shape, 0)
    lane = lambda shape: lax.broadcasted_iota(jnp.int32, shape, 1)

    @pl.loop(0, views)
    def _(v):
        s = (nz, 128)
        depth = banded(kd_ref, v, lane(s) - row(s), hz)
        zf[pl.ds(v * nz, nz), :] = depth
        high, low = split(depth)
        zl[pl.ds(v * nz, nz), 0:128] = high
        zl[pl.ds(v * nz, nz), 128:256] = high
        zl[pl.ds(v * nz, nz), 256:384] = low
        s = (ny, 256)
        rows = banded(kr_ref, v, (lane(s) & 63) - 1 - row(s), hy)
        high, low = split(rows)
        yf[v] = jnp.where(lane(s) < 128, high.astype(F32), low.astype(F32)).astype(BF16)
        s = (64, 128)
        rows = banded(kr_ref, v, row(s) - 1 - (lane(s) & 31), hy)
        high, low = split(rows)
        ya[v] = jnp.where(lane(s) < 64, high.astype(F32), low.astype(F32)).astype(BF16)
        s = (128, 128)
        shift = (hx - 1) // 2 + off_ref[0, v]
        for ref, sign in ((xf, 1), (xa, -1)):
            columns = banded(kc_ref, v, sign * (row(s) - lane(s)) + shift, hx)
            high, low = split(columns)
            ref[v, 0:128, 0:128] = high
            ref[v, 128:256, 0:128] = high
            ref[v, 0:128, 128:256] = low
            ref[v, 128:256, 128:256] = low

    kk = views * nz
    stack[...] = jnp.zeros_like(stack)
    for yb in range(3):
        @pl.loop(0, views)
        def _(v):
            s = (nz, 128)
            weights = []
            for zb in range(3):
                block = jnp.clip(g + zb - 1, 0, n_gz - 1) * n_xy + jnp.clip(r + yb - 1, 0, n_xy - 1)
                count = jnp.float32(0.0)
                for k in range(3):
                    count = count + jnp.where(bv_ref[block, k] == v, 1.0, 0.0)
                weights.append(count / 3.0)
            field = jnp.where(
                lane(s) < rz_n, weights[0], jnp.where(lane(s) < top, weights[1], weights[2])
            )
            scaled = zf[pl.ds(v * nz, nz), :] * field
            high, low = split(scaled)
            stack[pl.ds(v * nz, nz), :] = high.astype(F32)
            stack[pl.ds(kk + v * nz, nz), :] = high.astype(F32)
            stack[pl.ds(2 * kk + v * nz, nz), :] = low.astype(F32)

        for part in range(stack.shape[0] // 128):
            piece = stack[part * 128:(part + 1) * 128, :].T
            zt[yb, :, part * 128:(part + 1) * 128] = piece[0:112].astype(BF16)


    def depth_forward(y0):
        pair = jnp.concatenate(
            [ext[:, y0 + n, :] for n in range(2)], axis=1
        )
        high, low = split(pair)
        gap = jnp.zeros((16, 256), BF16)
        first = jnp.concatenate([high, gap, low, gap], axis=0)
        second = jnp.concatenate([high, gap], axis=0)
        result = jnp.dot(zl[:, 0:256], first, preferred_element_type=F32)
        result = result + jnp.dot(zl[:, 256:384], second, preferred_element_type=F32)
        for n in range(2):
            mid[:, y0 + n, :] = result[:, n * 128:(n + 1) * 128]

    def depth_adjoint(y0, yb):
        pair = jnp.concatenate(
            [mid[:, y0 + n, :] for n in range(2)], axis=1
        )
        high, low = split(pair)
        gap = jnp.zeros((stack.shape[0] - 3 * kk, 256), BF16)
        operand = jnp.concatenate([high, low, high, gap], axis=0)
        result = jnp.dot(zt[yb], operand, preferred_element_type=F32)
        for n in range(2):
            cor[:, y0 + n, :] = result[:, n * 128:(n + 1) * 128]

    group = 16

    def middle(v, z0):
        planes = []
        for p in range(group // 2):
            base = v * nz + z0 + 2 * p
            pair = jnp.concatenate([mid[base], mid[base + 1]], axis=1)
            high, low = split(pair)
            result = jnp.dot(
                yf[v, :, 0:192], jnp.concatenate([high, low, high], axis=0), preferred_element_type=F32
            )
            planes += [result[:, 0:128], result[:, 128:256]]
        data = jnp.concatenate(planes, axis=0)
        both = jnp.dot(jnp.concatenate(split(data), axis=1), xf[v], preferred_element_type=F32)
        blurred = both[:, 0:128] + both[:, 128:256]
        quotient = obs[v, pl.ds(z0, group)].reshape(group * ny, 128) / blurred
        both = jnp.dot(jnp.concatenate(split(quotient), axis=1), xa[v], preferred_element_type=F32)
        back = both[:, 0:128] + both[:, 128:256]
        for p in range(group // 2):
            base = v * nz + z0 + 2 * p
            pair = jnp.concatenate(
                [back[(2 * p) * ny:(2 * p + 1) * ny], back[(2 * p + 1) * ny:(2 * p + 2) * ny]], axis=1
            )
            high, low = split(pair)
            result = jnp.dot(
                ya[v, :, 0:96], jnp.concatenate([high, low, high], axis=0), preferred_element_type=F32
            )
            mid[base] = result[:, 0:128]
            mid[base + 1] = result[:, 128:256]

    groups = nz // group

    @pl.loop(0, ITERS)
    def _(step):
        @pl.when(step > 0)
        def _():
            begin(fy)
            begin(fz)

        await_all(fy)
        begin(fc)
        await_all(fz)

        @pl.loop(0, cols)
        def _(p):
            depth_forward(16 + 2 * p)

        await_all(fc)

        @pl.loop(0, 8)
        def _(p):
            depth_forward(2 * p)
            depth_forward(16 + ny + 2 * p)

        drain(fy)
        drain(fz)
        drain(fc)

        @pl.when(step == 0)
        def _():
            loads[2].wait()

        @pl.loop(0, halfv * groups)
        def _(i):
            middle(i // groups, (i % groups) * group)

        @pl.when(step == 0)
        def _():
            for d in range(1, n_xy):
                turn(d).wait()
            per = 128 // n_xy

            @pl.loop(0, halfv * octets)
            def _(i):
                parts = [recv[j, i] for j in range(n_xy)]
                place = lane((ny, 128)) // per
                for d in (4, 2, 1):
                    upper = (place & d) != 0
                    for a in range(n_xy):
                        if a & d:
                            continue
                        first, second = parts[a], parts[a + d]
                        parts[a] = jnp.where(upper, pltpu.roll(second, per * d, 1), first)
                        parts[a + d] = jnp.where(upper, second, pltpu.roll(first, 128 - per * d, 1))
                for j in range(n_xy):
                    obs[halfv + i // octets, (i % octets) * 8 + j] = parts[j]

        @pl.loop(0, (views - halfv) * groups)
        def _(i):
            middle(halfv + i // groups, (i % groups) * group)

        @pl.loop(0, 8)
        def _(p):
            depth_adjoint(2 * p, 0)
            depth_adjoint(16 + ny + 2 * p, 2)

        begin(ac)

        @pl.loop(0, cols)
        def _(p):
            depth_adjoint(16 + 2 * p, 1)

        begin(az)
        await_all(ac)

        def add_depth(y0, width):
            for n, z0, way in ((0, rz_n, "zd"), (1, top - rz_n, "zu")):
                @pl.when(has[way])
                def _():
                    @pl.loop(0, rz_n)
                    def _(i):
                        at = pl.ds(y0, width)
                        cor[z0 + i, at, :] = cor[z0 + i, at, :] + rz[n, i, at, :]

        add_depth(0, 16)
        add_depth(16 + ny, 16)
        begin(ay)
        await_all(az)
        add_depth(16, ny)
        await_all(ay)
        for n, y0, way in ((0, 16, "yd"), (1, ny, "yu")):
            @pl.when(has[way])
            def _():
                @pl.loop(0, nz)
                def _(i):
                    at = pl.ds(y0, 16)
                    cor[rz_n + i, at, :] = cor[rz_n + i, at, :] + ry[n, i]

        @pl.loop(0, nz)
        def _(i):
            at = pl.ds(16, ny)
            fresh = ext[rz_n + i, at, :] * cor[rz_n + i, at, :]
            ext[rz_n + i, at, :] = fresh
            out_ref[i] = fresh

        drain(ac)
        drain(az)
        drain(ay)


def solution(mesh):
    n_gz, n_xy = mesh.shape["gz"], mesh.shape["xy"]

    def local(est, upright, turned, kd, kr, kc, offsets, block_views):
        nz, ny, nx = est.shape
        views, hz = kd.shape
        hy, hx = kr.shape[1], kc.shape[1]
        halfv = upright.shape[0]
        kk = views * nz
        stacked = -(-3 * kk // 128) * 128
        dma = pltpu.SemaphoreType.DMA
        vmem = pltpu.VMEM
        smem = pl.BlockSpec(memory_space=pltpu.SMEM)
        anyspace = pl.BlockSpec(memory_space=pl.ANY)
        octets = halfv * (nz // 8)
        rz_n = (hz - 1) // 2
        return pl.pallas_call(
            functools.partial(kernel, nz, ny, views, halfv, n_gz, n_xy, hz, hy, hx),
            out_shape=jax.ShapeDtypeStruct((nz, ny, nx), F32),
            in_specs=[smem] * 5 + [anyspace] * 3,
            out_specs=pl.BlockSpec(memory_space=pltpu.VMEM),
            scratch_shapes=[
                vmem((112, 64, 128), F32),
                vmem((kk, 64, 128), F32),
                vmem((112, 64, 128), F32),
                vmem((2, rz_n, 64, 128), F32),
                vmem((2, nz, 16, 128), F32),
                vmem((views, nz, ny, 128), F32),
                vmem(turned.shape, F32),
                vmem((n_xy, octets, ny, 128), F32),
                vmem((n_xy, octets, ny, 128), F32),
                vmem((kk, 384), BF16),
                vmem((kk, 128), F32),
                vmem((stacked, 128), F32),
                vmem((3, 112, stacked), BF16),
                vmem((views, ny, 256), BF16),
                vmem((views, 64, 128), BF16),
                vmem((views, 256, 256), BF16),
                vmem((views, 256, 256), BF16),
                dma((3,)),
                dma((2,)), dma((2,)), dma((2,)), dma((2,)), dma((4,)), dma((4,)),
                dma((2,)), dma((2,)), dma((4,)), dma((4,)), dma((2,)), dma((2,)),
                dma((n_xy - 1,)), dma((n_xy - 1,)),
            ],
            compiler_params=pltpu.CompilerParams(
                collective_id=0, has_side_effects=True, vmem_limit_bytes=60 * 1024 * 1024
            ),
            name="deconvolve",
        )(kd, kr, kc, offsets.reshape(1, views), block_views, est, upright, turned)

    in_specs = (
        P("gz", "xy", None),
        P(None, "gz", "xy", None),
        P(None, "gz", "xy", None),
        P(), P(), P(), P(), P(),
    )
    return jax.shard_map(
        local, mesh=mesh, in_specs=in_specs, out_specs=P("gz", "xy", None), check_vma=False
    )
```

time: 552 us -> 172 us (0.31)
  the two profiles are of different devices: /device:TPU:31 before, /device:TPU:7 now
where the time goes in v1:
time: 172 us; the launch traced here: 170 us
  Pallas kernels  167 us (97%)
  local copies, waits for them, and re-layouts  3.48 us (2%)
    pallas_call x1, Pallas kernels, local(): pl.pallas_call(functools.partial(kernel, nz, ny, views, halfv, n_gz, n_xy...  167 us
    unnamed x2, local copies, waits for them, and re-layouts  3.48 us

profile of v1, /device:TPU:7, one launch (start us, length us, event | category | flops | bytes accessed | tf_op | source)
XLA Modules:
  0.0 170.2 jit_solution(16743143498934608712)
XLA Ops:
  0.0 1.4 copy.9.bv_ref
  1.4 166.7 %deconvolve.1 = f32[48,32,128]{2,1,0:T(8,128)} custom-call(f32[6,61]{1,0:T(8,128)} %kd_ref.1, f32[6,31]{1,0:T(8,128)} %kr_ref.1, f32[6,31]{1,0:T(8,128)} %kc_ref.1, s32[1,6]{1,0:T(1,128)} %bitcast.1, s32[128,3]{1,0:T(8,128)} %copy.9.bv_ref, f32[48,32,128]{2,1,0:T(8,128)} %est_hbm.1, f32[3,48,32,128]{3,2,1,0:T(8,128)} %up_hbm.1, f32[3,48,16,256]{3,2,1,0:T(8,128)} %vt_hbm.1), custom_call_target="tpu_custom_call" | custom-call | tf_op jit(solution)/shard_map/deconvolve/pallas_call | solution.py:431
  168.1 2.1 %copy.11 = f32[48,32,128]{2,1,0:T(8,128)} copy(f32[48,32,128]{2,1,0:T(8,128)} %deconvolve.1) | data formatting | bytes 1572864

commit v2 on v1

v2 whole, which is shorter than its diff:
```python
import functools

import jax
import jax.numpy as jnp
from jax import lax
from jax.experimental import pallas as pl
from jax.experimental.pallas import tpu as pltpu
from jax.sharding import PartitionSpec as P

ITERS = 2
PITCH = 66
F32 = jnp.float32
BF16 = jnp.bfloat16
MESH = pl.DeviceIdType.MESH


def split(value):
    high = value.astype(BF16)
    low = (value - high.astype(F32)).astype(BF16)
    return high, low


def row(shape):
    return lax.broadcasted_iota(jnp.int32, shape, 0)


def lane(shape):
    return lax.broadcasted_iota(jnp.int32, shape, 1)


def kernel(
    nz, ny, views, halfv, n_gz, n_xy, hz, hy, hx,
    off_ref, kd_ref, kr_ref, kc_ref, bv_ref, est_hbm, up_hbm, vt_hbm,
    out_ref,
    ext, rim, wide, mid, cor, sc, sz, sy, rc, rz, ry, obs, vt, pack, recv,
    taps, stack, flat, zl, zt, yf, ya, xf, xa, ahead, ratio, behind,
    load_sem, fz_send, fz_recv, fy_send, fy_recv, fc_send, fc_recv,
    az_send, az_recv, ac_send, ac_recv, ay_send, ay_recv, t_send, t_recv,
):
    g = lax.axis_index("gz")
    r = lax.axis_index("xy")
    rz_n = (hz - 1) // 2
    top = rz_n + nz
    kk = views * nz
    only = nz - rz_n
    spans = ((only, rz_n), (0, only), (rz_n, nz))
    has = {"zu": g < n_gz - 1, "zd": g > 0, "yu": r < n_xy - 1, "yd": r > 0}
    opposite = {"zu": "zd", "zd": "zu", "yu": "yd", "yd": "yu"}
    target = {"zu": {"gz": g + 1}, "zd": {"gz": g - 1}, "yu": {"xy": r + 1}, "yd": {"xy": r - 1}}

    loads = [
        pltpu.make_async_copy(est_hbm, ext.at[pl.ds(rz_n, nz)], load_sem.at[0]),
        pltpu.make_async_copy(vt_hbm, vt, load_sem.at[1]),
        pltpu.make_async_copy(up_hbm, obs.at[pl.ds(0, halfv)], load_sem.at[2]),
    ]
    for load in loads:
        load.start()

    barrier = pltpu.get_barrier_semaphore()
    for d in range(1, n_xy):
        pl.semaphore_signal(
            barrier, inc=1, device_id={"xy": lax.rem(r + d, n_xy)}, device_id_type=MESH
        )
    for way in ("zu", "zd"):
        @pl.when(has[way])
        def _():
            pl.semaphore_signal(barrier, inc=1, device_id=target[way], device_id_type=MESH)

    def clear(z0, z1, y0, y1, refs):
        @pl.loop(z0, z1)
        def _(i):
            for ref in refs:
                ref[i, pl.ds(y0, y1 - y0), :] = jnp.zeros((y1 - y0, 128), F32)

    clear(top + rz_n, ext.shape[0], 0, ny, (ext, rim))

    @pl.when(jnp.logical_not(has["zd"]))
    def _():
        clear(0, rz_n, 0, ny, (ext, rim))

    @pl.when(jnp.logical_not(has["zu"]))
    def _():
        clear(top, top + rz_n, 0, ny, (ext, rim))

    @pl.when(jnp.logical_not(has["yd"]))
    def _():
        clear(rz_n, top, 0, 16, (rim,))

    @pl.when(jnp.logical_not(has["yu"]))
    def _():
        clear(rz_n, top, 16, 32, (rim,))

    def flow(way, src, dst, send, recv_sem, number):
        def make():
            return pltpu.make_async_remote_copy(
                src_ref=src, dst_ref=dst, send_sem=send.at[number], recv_sem=recv_sem.at[number],
                device_id=target[way], device_id_type=MESH,
            )

        def start():
            @pl.when(has[way])
            def _():
                make().start()

        def arrived():
            @pl.when(has[opposite[way]])
            def _():
                make().wait_recv()

        def sent():
            @pl.when(has[way])
            def _():
                make().wait_send()

        return start, arrived, sent

    def rows(ref, z0, z1):
        return ref.at[pl.ds(z0, z1 - z0)]

    def cut(ref, z0, z1, y0):
        return ref.at[pl.ds(z0, z1 - z0), pl.ds(y0, 16), :]

    fz = [
        flow("zu", rows(ext, top - rz_n, top), rows(ext, 0, rz_n), fz_send, fz_recv, 0),
        flow("zd", rows(ext, rz_n, 2 * rz_n), rows(ext, top, top + rz_n), fz_send, fz_recv, 1),
    ]
    fy = []
    for n, (a, b) in enumerate(spans):
        a, b = rz_n + a, rz_n + b
        fy.append([
            flow("yu", cut(ext, a, b, ny - 16), cut(rim, a, b, 0), fy_send, fy_recv, 2 * n),
            flow("yd", cut(ext, a, b, 0), cut(rim, a, b, 16), fy_send, fy_recv, 2 * n + 1),
        ])
    fc = [
        [
            flow("zu", rows(rim, rz_n + only, 2 * rz_n), rows(rim, 0, rz_n - only), fc_send, fc_recv, 0),
            flow("zd", rows(rim, rz_n + only, 2 * rz_n), rows(rim, top + only, top + rz_n), fc_send, fc_recv, 1),
        ],
        [flow("zd", rows(rim, rz_n, rz_n + only), rows(rim, top, top + only), fc_send, fc_recv, 2)],
        [flow("zu", rows(rim, 2 * rz_n, top), rows(rim, rz_n - only, rz_n), fc_send, fc_recv, 3)],
    ]
    ac = [
        [flow("zu", rows(sc.at[0], 0, only), rows(rc.at[0], 0, only), ac_send, ac_recv, 0)],
        [flow("zd", rows(sc.at[1], rz_n - only, rz_n), rows(rc.at[1], rz_n - only, rz_n), ac_send, ac_recv, 1)],
        [
            flow("zu", rows(sc.at[0], only, rz_n), rows(rc.at[0], only, rz_n), ac_send, ac_recv, 2),
            flow("zd", rows(sc.at[1], 0, rz_n - only), rows(rc.at[1], 0, rz_n - only), ac_send, ac_recv, 3),
        ],
    ]
    az = [
        flow("zu", sz.at[0], rz.at[0], az_send, az_recv, 0),
        flow("zd", sz.at[1], rz.at[1], az_send, az_recv, 1),
    ]
    ay = []
    for n, (a, b) in enumerate((spans[1], spans[2], spans[0])):
        ay.append([
            flow("yu", rows(sy.at[0], a, b), rows(ry.at[0], a, b), ay_send, ay_recv, 2 * n),
            flow("yd", rows(sy.at[1], a, b), rows(ry.at[1], a, b), ay_send, ay_recv, 2 * n + 1),
        ])

    def begin(flows):
        for f in flows:
            f[0]()

    def await_all(flows):
        for f in flows:
            f[1]()

    def drain(flows):
        for f in flows:
            f[2]()

    loads[0].wait()
    greeted = n_xy - 1 + has["zu"].astype(jnp.int32) + has["zd"].astype(jnp.int32)
    pl.semaphore_wait(barrier, greeted)
    for part in fy:
        begin(part)
    begin(fz)

    loads[1].wait()
    octets = nz // 8

    @pl.loop(0, halfv * octets)
    def _(i):
        block = vt[i // octets, pl.ds((i % octets) * 8, 8)].reshape(128, ny * n_xy)
        for half in range(2):
            part = block[:, half * 128:(half + 1) * 128].T
            for piece in range(128 // ny):
                pack[half * (128 // ny) + piece, i] = part[piece * ny:(piece + 1) * ny]

    def turn(d):
        peer = lax.rem(r + d, n_xy)
        return pltpu.make_async_remote_copy(
            src_ref=pack.at[peer], dst_ref=recv.at[r], send_sem=t_send.at[d - 1], recv_sem=t_recv.at[d - 1],
            device_id={"xy": peer}, device_id_type=MESH,
        )

    for d in range(1, n_xy):
        turn(d).start()

    @pl.loop(0, halfv * octets)
    def _(i):
        recv[r, i] = pack[r, i]

    taps[...] = jnp.zeros_like(taps)
    for n, ref in enumerate((kd_ref, kr_ref, kc_ref)):
        value = ref[...]
        value = value / jnp.sum(value, axis=1, keepdims=True)
        taps[n, 0:views, 0:value.shape[1]] = value
        if n == 1:
            taps[n, 0:views, 64:64 + value.shape[1]] = value
    stack[...] = jnp.zeros_like(stack)

    @pl.loop(0, views)
    def _(v):
        def toeplitz(line, count, shift):
            return pltpu.roll(jnp.broadcast_to(line, (count, 128)), shift, 1, stride=1, stride_axis=0)

        depth = toeplitz(taps[0, pl.ds(v, 1), :], nz, 0)
        for n in range(3):
            stack[pl.ds(n * kk + v * nz, nz), :] = depth
        high, low = split(depth)
        zl[pl.ds(v * nz, nz), 0:128] = high
        zl[pl.ds(v * nz, nz), 128:256] = high
        zl[pl.ds(v * nz, nz), 256:384] = low

        line = toeplitz(taps[1, pl.ds(v, 1), :], ny, 1)
        high, low = split(line)
        yf[v, :, 0:128] = high
        yf[v, :, 128:256] = low
        line = jnp.concatenate([line] * (128 // ny), axis=0).T[0:64]
        high, low = split(line)
        ya[v] = jnp.where(lane((64, 128)) < 64, high.astype(F32), low.astype(F32)).astype(BF16)

        s = (128, 128)
        reach = (hx - 1) // 2
        shift = off_ref[0, v] + reach
        tap = lane(s) - row(s) + shift
        line = pltpu.roll(jnp.broadcast_to(taps[2, pl.ds(v, 1), :], (8, 128)), 128 - shift, 1)[0:1]
        column = jnp.where((tap >= 0) & (tap < hx), toeplitz(line, 128, 0), 0.0)
        for ref, matrix in ((xa, column), (xf, column.T)):
            high, low = split(matrix)
            ref[v, 0:128, 0:128] = high
            ref[v, 128:256, 0:128] = high
            ref[v, 0:128, 128:256] = low
            ref[v, 128:256, 128:256] = low

    for part in range(stack.shape[0] // 128):
        flat[:, part * 128:(part + 1) * 128] = stack[part * 128:(part + 1) * 128, :].T[0:112]

    for yb in range(3):
        fields = []
        for zb in range(3):
            block = jnp.clip(g + zb - 1, 0, n_gz - 1) * n_xy + jnp.clip(r + yb - 1, 0, n_xy - 1)
            chosen = bv_ref[pl.ds(block, 1), :]
            view = lax.rem(lane((1, stack.shape[0])), kk) // nz
            field = jnp.zeros((1, stack.shape[0]), F32)
            for k in range(bv_ref.shape[1]):
                one = jnp.broadcast_to(chosen[:, k:k + 1], (1, stack.shape[0]))
                field = field + jnp.where(one == view, 1.0, 0.0)
            fields.append(field / float(bv_ref.shape[1]))

        for i in range(7):
            s = (16, stack.shape[0])
            number = row(s) + 16 * i
            field = jnp.where(number < rz_n, fields[0], jnp.where(number < top, fields[1], fields[2]))
            scaled = flat[16 * i:16 * i + 16, :] * field
            high, low = split(scaled)
            high, low = high.astype(F32), low.astype(F32)
            chosen = jnp.where(lane(s) < 2 * kk, high, low)
            zt[yb, 16 * i:16 * i + 16, :] = chosen.astype(BF16)

    def widen(source, z0, z1, y0, width, to):
        @pl.loop(z0, z1)
        def _(i):
            wide[pl.ds(i * PITCH + to, width), :] = source[i, pl.ds(y0, width), :]

    def widen_rim(z0, z1):
        widen(rim, z0, z1, 0, 16, 0)
        widen(rim, z0, z1, 16, 16, 16 + ny)

    def depth_forward(y0):
        pair = jnp.concatenate(
            [wide[pl.ds(y0 + n, 112, stride=PITCH), :] for n in range(2)], axis=1
        )
        high, low = split(pair)
        gap = jnp.zeros((16, 256), BF16)
        first = jnp.concatenate([high, gap, low, gap], axis=0)
        second = jnp.concatenate([high, gap], axis=0)
        result = jnp.dot(zl[:, 0:256], first, preferred_element_type=F32)
        result = result + jnp.dot(zl[:, 256:384], second, preferred_element_type=F32)
        for n in range(2):
            mid[pl.ds(y0 + n, kk, stride=PITCH), :] = result[:, n * 128:(n + 1) * 128]

    def depth_adjoint(y0, yb):
        pair = jnp.concatenate(
            [mid[pl.ds(y0 + n, kk, stride=PITCH), :] for n in range(2)], axis=1
        )
        high, low = split(pair)
        gap = jnp.zeros((stack.shape[0] - 3 * kk, 256), BF16)
        operand = jnp.concatenate([high, low, high, gap], axis=0)
        result = jnp.dot(zt[yb], operand, preferred_element_type=F32)
        for n in range(2):
            cor[pl.ds(y0 + n, 112, stride=PITCH), :] = result[:, n * 128:(n + 1) * 128]

    group = 16
    groups = nz // group

    def middle(step):
        spare = views * nz
        count = views * groups

        @pl.loop(0, count + 3)
        def _(i):
            @pl.when((step == 0) & (i == halfv * groups))
            def _():
                unpack()

            def at(stage):
                number = jnp.clip(i - stage, 0, count - 1)
                return number // groups, (number % groups) * group

            v, z0 = at(3)
            base = jnp.where(i < 3, spare, v * nz + z0) * PITCH
            for p in range(group // 2):
                operand = jnp.concatenate([behind[p], behind[p, 0:ny]], axis=0)
                result = jnp.dot(ya[v, :, 0:96], operand, preferred_element_type=F32)
                mid[pl.ds(base + 2 * p * PITCH, 64), :] = result[:, 0:128]
                mid[pl.ds(base + (2 * p + 1) * PITCH, 64), :] = result[:, 128:256]

            v, z0 = at(2)
            both = jnp.dot(ratio[...], xa[v], preferred_element_type=F32)
            back = both[:, 0:128] + both[:, 128:256]
            for p in range(group // 2):
                pair = jnp.concatenate(
                    [back[(2 * p) * ny:(2 * p + 1) * ny], back[(2 * p + 1) * ny:(2 * p + 2) * ny]], axis=1
                )
                behind[p] = jnp.concatenate(split(pair), axis=0)

            v, z0 = at(1)
            both = jnp.dot(ahead[...], xf[v], preferred_element_type=F32)
            blurred = both[:, 0:128] + both[:, 128:256]
            quotient = obs[v, pl.ds(z0, group)].reshape(group * ny, 128) / blurred
            ratio[...] = jnp.concatenate(split(quotient), axis=1)

            v, z0 = at(0)
            base = (v * nz + z0) * PITCH
            for p in range(group // 2):
                pair = jnp.concatenate(
                    [mid[pl.ds(base + (2 * p + n) * PITCH, 64), :] for n in range(2)], axis=1
                )
                high, low = split(pair)
                result = jnp.dot(
                    yf[v, :, 0:192], jnp.concatenate([high, low, high], axis=0), preferred_element_type=F32
                )
                for n in range(2):
                    ahead[(2 * p + n) * ny:(2 * p + n + 1) * ny, :] = jnp.concatenate(
                        split(result[:, n * 128:(n + 1) * 128]), axis=1
                    )

    def unpack():
        for d in range(1, n_xy):
            turn(d).wait()
        per = 128 // n_xy

        @pl.loop(0, halfv * octets)
        def _(i):
            parts = [recv[j, i] for j in range(n_xy)]
            place = lane((ny, 128)) // per
            for d in (4, 2, 1):
                upper = (place & d) != 0
                for a in range(n_xy):
                    if a & d:
                        continue
                    first, second = parts[a], parts[a + d]
                    parts[a] = jnp.where(upper, pltpu.roll(second, per * d, 1), first)
                    parts[a + d] = jnp.where(upper, second, pltpu.roll(first, 128 - per * d, 1))
            for j in range(n_xy):
                obs[halfv + i // octets, (i % octets) * 8 + j] = parts[j]

    def add_depth(source, n, z0, i0, i1, pieces, way):
        @pl.when(has[way])
        def _():
            @pl.loop(i0, i1)
            def _(i):
                for y0, width, to in pieces:
                    at = pl.ds((rz_n + z0 + i) * PITCH + to, width)
                    cor[at, :] = cor[at, :] + source[n, i, pl.ds(y0, width), :]

    sides = ((0, 16, 0), (16, 16, 16 + ny))
    whole = ((0, ny, 16),)

    def give(n):
        a, b = (spans[1], spans[2], spans[0])[n]

        @pl.loop(a, b)
        def _(i):
            sy[0, i] = cor[pl.ds((rz_n + i) * PITCH + 16 + ny, 16), :]
            sy[1, i] = cor[pl.ds((rz_n + i) * PITCH, 16), :]

        begin(ay[n])

    @pl.loop(0, ITERS)
    def _(step):
        @pl.when(step > 0)
        def _():
            for part in fy:
                begin(part)
            begin(fz)

        widen(ext, rz_n, top, 0, ny, 16)
        for n in range(3):
            await_all(fy[n])
            begin(fc[n])
        widen_rim(rz_n, top)
        await_all(fz)
        widen(ext, 0, rz_n, 0, ny, 16)
        widen(ext, top, ext.shape[0], 0, ny, 16)

        @pl.loop(0, ny // 4)
        def _(p):
            depth_forward(16 + 4 * p)
            depth_forward(18 + 4 * p)

        for n in range(3):
            await_all(fc[n])
        widen_rim(0, rz_n)
        widen_rim(top, ext.shape[0])

        @pl.loop(0, 8)
        def _(p):
            depth_forward(2 * p)
            depth_forward(16 + ny + 2 * p)

        for n in range(3):
            drain(fy[n])
            drain(fc[n])
        drain(fz)

        @pl.when(step == 0)
        def _():
            loads[2].wait()

        middle(step)

        @pl.loop(0, 8)
        def _(p):
            depth_adjoint(2 * p, 0)
            depth_adjoint(16 + ny + 2 * p, 2)

        def pick(dest, y0, width, to):
            @pl.loop(0, rz_n)
            def _(i):
                dest[0, i, pl.ds(to, width), :] = cor[pl.ds((top + i) * PITCH + y0, width), :]
                dest[1, i, pl.ds(to, width), :] = cor[pl.ds(i * PITCH + y0, width), :]

        pick(sc, 0, 16, 0)
        pick(sc, 16 + ny, 16, 16)
        for part in ac:
            begin(part)

        @pl.loop(0, ny // 4)
        def _(p):
            depth_adjoint(16 + 4 * p, 1)
            depth_adjoint(18 + 4 * p, 1)

        pick(sz, 16, ny, 0)
        begin(az)
        await_all(ac[0])
        add_depth(rc, 0, 0, 0, only, sides, "zd")
        give(0)
        await_all(ac[1])
        add_depth(rc, 1, only, rz_n - only, rz_n, sides, "zu")
        give(1)
        await_all(ac[2])
        add_depth(rc, 0, 0, only, rz_n, sides, "zd")
        add_depth(rc, 1, only, 0, rz_n - only, sides, "zu")
        give(2)
        await_all(az)
        add_depth(rz, 0, 0, 0, rz_n, whole, "zd")
        add_depth(rz, 1, only, 0, rz_n, whole, "zu")
        for part in ay:
            await_all(part)
        for n, y0, way in ((0, 16, "yd"), (1, ny, "yu")):
            @pl.when(has[way])
            def _():
                @pl.loop(0, nz)
                def _(i):
                    at = pl.ds((rz_n + i) * PITCH + y0, 16)
                    cor[at, :] = cor[at, :] + ry[n, i]

        @pl.loop(0, nz)
        def _(i):
            fresh = ext[rz_n + i] * cor[pl.ds((rz_n + i) * PITCH + 16, ny), :]
            ext[rz_n + i] = fresh
            out_ref[i] = fresh

        for n in range(3):
            drain(ac[n])
            drain(ay[n])
        drain(az)


def solution(mesh):
    n_gz, n_xy = mesh.shape["gz"], mesh.shape["xy"]

    def local(est, upright, turned, kd, kr, kc, offsets, block_views):
        nz, ny, nx = est.shape
        views, hz = kd.shape
        hy, hx = kr.shape[1], kc.shape[1]
        halfv = upright.shape[0]
        kk = views * nz
        stacked = -(-3 * kk // 128) * 128
        dma = pltpu.SemaphoreType.DMA
        vmem = pltpu.VMEM
        smem = pl.BlockSpec(memory_space=pltpu.SMEM)
        vspace = pl.BlockSpec(memory_space=pltpu.VMEM)
        anyspace = pl.BlockSpec(memory_space=pl.ANY)
        octets = halfv * (nz // 8)
        rz_n = (hz - 1) // 2
        return pl.pallas_call(
            functools.partial(kernel, nz, ny, views, halfv, n_gz, n_xy, hz, hy, hx),
            out_shape=jax.ShapeDtypeStruct((nz, ny, nx), F32),
            in_specs=[smem] + [vspace] * 4 + [anyspace] * 3,
            out_specs=vspace,
            scratch_shapes=[
                vmem((112, ny, 128), F32),
                vmem((112, 32, 128), F32),
                vmem((112 * PITCH, 128), F32),
                vmem(((kk + 16) * PITCH, 128), F32),
                vmem((112 * PITCH, 128), F32),
                vmem((2, rz_n, 32, 128), F32),
                vmem((2, rz_n, ny, 128), F32),
                vmem((2, nz, 16, 128), F32),
                vmem((2, rz_n, 32, 128), F32),
                vmem((2, rz_n, ny, 128), F32),
                vmem((2, nz, 16, 128), F32),
                vmem((views, nz, ny, 128), F32),
                vmem(turned.shape, F32),
                vmem((n_xy, octets, ny, 128), F32),
                vmem((n_xy, octets, ny, 128), F32),
                vmem((3, 8, 128), F32),
                vmem((stacked, 128), F32),
                vmem((112, stacked), F32),
                vmem((kk, 384), BF16),
                vmem((3, 112, stacked), BF16),
                vmem((views, ny, 256), BF16),
                vmem((views, 64, 128), BF16),
                vmem((views, 256, 256), BF16),
                vmem((views, 256, 256), BF16),
                vmem((16 * ny, 256), BF16),
                vmem((16 * ny, 256), BF16),
                vmem((8, 2 * ny, 256), BF16),
                dma((3,)),
                dma((2,)), dma((2,)), dma((6,)), dma((6,)), dma((4,)), dma((4,)),
                dma((2,)), dma((2,)), dma((4,)), dma((4,)), dma((6,)), dma((6,)),
                dma((n_xy - 1,)), dma((n_xy - 1,)),
            ],
            compiler_params=pltpu.CompilerParams(
                collective_id=0, has_side_effects=True, vmem_limit_bytes=60 * 1024 * 1024
            ),
            name="deconvolve",
        )(offsets.reshape(1, views), kd, kr, kc, block_views, est, upright, turned)

    in_specs = (
        P("gz", "xy", None),
        P(None, "gz", "xy", None),
        P(None, "gz", "xy", None),
        P(), P(), P(), P(), P(),
    )
    return jax.shard_map(
        local, mesh=mesh, in_specs=in_specs, out_specs=P("gz", "xy", None), check_vma=False
    )
```

time: 172 us -> 150 us (0.87)
  Pallas kernels: 167 us -> 146 us
    pallas_call x1, Pallas kernels: 167 us -> 146 us  [local(): pl.pallas_call(functools.partial(kernel, nz, ny, views, halfv, n_gz, n_xy...]
where the time goes in v2:
time: 150 us; the launch traced here: 149 us
  Pallas kernels  146 us (97%)
  local copies, waits for them, and re-layouts  3.48 us (2%)
    pallas_call x1, Pallas kernels, local(): pl.pallas_call(functools.partial(kernel, nz, ny, views, halfv, n_gz, n_xy...  146 us
    unnamed x2, local copies, waits for them, and re-layouts  3.48 us

profile of v2, /device:TPU:7, one launch (start us, length us, event | category | flops | bytes accessed | tf_op | source)
XLA Modules:
  0.0 149.3 jit_solution(14987981477585879839)
XLA Ops:
  0.0 1.4 copy.9.bv_ref
  1.4 145.8 %deconvolve.1 = f32[48,32,128]{2,1,0:T(8,128)} custom-call(s32[1,6]{1,0:T(1,128)} %bitcast.1, f32[6,61]{1,0:T(8,128)} %kd_ref.1, f32[6,31]{1,0:T(8,128)} %kr_ref.1, f32[6,31]{1,0:T(8,128)} %kc_ref.1, s32[128,3]{1,0:T(8,128)} %copy.9.bv_ref, f32[48,32,128]{2,1,0:T(8,128)} %est_hbm.1, f32[3,48,32,128]{3,2,1,0:T(8,128)} %up_hbm.1, f32[3,48,16,256]{3,2,1,0:T(8,128)} %vt_hbm.1), custom_call_target="tpu_custom_call" | custom-call | tf_op jit(solution)/shard_map/deconvolve/pallas_call | solution.py:521
  147.2 2.1 %copy.11 = f32[48,32,128]{2,1,0:T(8,128)} copy(f32[48,32,128]{2,1,0:T(8,128)} %deconvolve.1) | data formatting | bytes 1572864

commit v3 on v2

--- a/solution.py
+++ b/solution.py
@@ -252,13 +252,14 @@
         fields = []
         for zb in range(3):
             block = jnp.clip(g + zb - 1, 0, n_gz - 1) * n_xy + jnp.clip(r + yb - 1, 0, n_xy - 1)
-            chosen = bv_ref[pl.ds(block, 1), :]
-            view = lax.rem(lane((1, stack.shape[0])), kk) // nz
+            held = lane(bv_ref.shape) == block
+            chosen = jnp.sum(jnp.where(held, bv_ref[...], 0).astype(F32), axis=1, keepdims=True)
+            view = (lax.rem(lane((1, stack.shape[0])), kk) // nz).astype(F32)
             field = jnp.zeros((1, stack.shape[0]), F32)
-            for k in range(bv_ref.shape[1]):
-                one = jnp.broadcast_to(chosen[:, k:k + 1], (1, stack.shape[0]))
+            for k in range(bv_ref.shape[0]):
+                one = jnp.broadcast_to(chosen[k:k + 1, :], (1, stack.shape[0]))
                 field = field + jnp.where(one == view, 1.0, 0.0)
-            fields.append(field / float(bv_ref.shape[1]))
+            fields.append(field / float(bv_ref.shape[0]))
 
         for i in range(7):
             s = (16, stack.shape[0])
@@ -271,7 +272,7 @@
             zt[yb, 16 * i:16 * i + 16, :] = chosen.astype(BF16)
 
     def widen(source, z0, z1, y0, width, to):
-        @pl.loop(z0, z1)
+        @pl.loop(z0, z1, unroll=6 if (z1 - z0) % 6 == 0 else 2)
         def _(i):
             wide[pl.ds(i * PITCH + to, width), :] = source[i, pl.ds(y0, width), :]
 
@@ -363,7 +364,7 @@
             turn(d).wait()
         per = 128 // n_xy
 
-        @pl.loop(0, halfv * octets)
+        @pl.loop(0, halfv * octets, unroll=2)
         def _(i):
             parts = [recv[j, i] for j in range(n_xy)]
             place = lane((ny, 128)) // per
@@ -381,7 +382,7 @@
     def add_depth(source, n, z0, i0, i1, pieces, way):
         @pl.when(has[way])
         def _():
-            @pl.loop(i0, i1)
+            @pl.loop(i0, i1, unroll=6 if (i1 - i0) % 6 == 0 else 2)
             def _(i):
                 for y0, width, to in pieces:
                     at = pl.ds((rz_n + z0 + i) * PITCH + to, width)
@@ -393,7 +394,7 @@
     def give(n):
         a, b = (spans[1], spans[2], spans[0])[n]
 
-        @pl.loop(a, b)
+        @pl.loop(a, b, unroll=6)
         def _(i):
             sy[0, i] = cor[pl.ds((rz_n + i) * PITCH + 16 + ny, 16), :]
             sy[1, i] = cor[pl.ds((rz_n + i) * PITCH, 16), :]
@@ -417,20 +418,21 @@
         widen(ext, 0, rz_n, 0, ny, 16)
         widen(ext, top, ext.shape[0], 0, ny, 16)
 
-        @pl.loop(0, ny // 4)
+        @pl.loop(0, ny // 8)
         def _(p):
-            depth_forward(16 + 4 * p)
-            depth_forward(18 + 4 * p)
+            for n in range(4):
+                depth_forward(16 + 8 * p + 2 * n)
 
         for n in range(3):
             await_all(fc[n])
         widen_rim(0, rz_n)
         widen_rim(top, ext.shape[0])
 
-        @pl.loop(0, 8)
+        @pl.loop(0, 4)
         def _(p):
-            depth_forward(2 * p)
-            depth_forward(16 + ny + 2 * p)
+            for n in range(2):
+                depth_forward(4 * p + 2 * n)
+                depth_forward(16 + ny + 4 * p + 2 * n)
 
         for n in range(3):
             drain(fy[n])
@@ -443,13 +445,14 @@
 
         middle(step)
 
-        @pl.loop(0, 8)
+        @pl.loop(0, 4)
         def _(p):
-            depth_adjoint(2 * p, 0)
-            depth_adjoint(16 + ny + 2 * p, 2)
+            for n in range(2):
+                depth_adjoint(4 * p + 2 * n, 0)
+                depth_adjoint(16 + ny + 4 * p + 2 * n, 2)
 
         def pick(dest, y0, width, to):
-            @pl.loop(0, rz_n)
+            @pl.loop(0, rz_n, unroll=6)
             def _(i):
                 dest[0, i, pl.ds(to, width), :] = cor[pl.ds((top + i) * PITCH + y0, width), :]
                 dest[1, i, pl.ds(to, width), :] = cor[pl.ds(i * PITCH + y0, width), :]
@@ -459,10 +462,10 @@
         for part in ac:
             begin(part)
 
-        @pl.loop(0, ny // 4)
+        @pl.loop(0, ny // 8)
         def _(p):
-            depth_adjoint(16 + 4 * p, 1)
-            depth_adjoint(18 + 4 * p, 1)
+            for n in range(4):
+                depth_adjoint(16 + 8 * p + 2 * n, 1)
 
         pick(sz, 16, ny, 0)
         begin(az)
@@ -484,12 +487,12 @@
         for n, y0, way in ((0, 16, "yd"), (1, ny, "yu")):
             @pl.when(has[way])
             def _():
-                @pl.loop(0, nz)
+                @pl.loop(0, nz, unroll=6)
                 def _(i):
                     at = pl.ds((rz_n + i) * PITCH + y0, 16)
                     cor[at, :] = cor[at, :] + ry[n, i]
 
-        @pl.loop(0, nz)
+        @pl.loop(0, nz, unroll=6)
         def _(i):
             fresh = ext[rz_n + i] * cor[pl.ds((rz_n + i) * PITCH + 16, ny), :]
             ext[rz_n + i] = fresh
@@ -560,7 +563,7 @@
                 collective_id=0, has_side_effects=True, vmem_limit_bytes=60 * 1024 * 1024
             ),
             name="deconvolve",
-        )(offsets.reshape(1, views), kd, kr, kc, block_views, est, upright, turned)
+        )(offsets.reshape(1, views), kd, kr, kc, block_views.T, est, upright, turned)
 
     in_specs = (
         P("gz", "xy", None),

time: 150 us -> 143 us (0.953)
  Pallas kernels: 146 us -> 141 us
    pallas_call x1, Pallas kernels: 146 us -> 141 us  [local(): pl.pallas_call(functools.partial(kernel, nz, ny, views, halfv, n_gz, n_xy...]
    unnamed x2 -> x1, local copies, waits for them, and re-layouts: 3.48 us -> 2.06 us
where the time goes in v3:
time: 143 us
  Pallas kernels  141 us (99%)
  local copies, waits for them, and re-layouts  2.06 us (1%)
    pallas_call x1, Pallas kernels, local(): pl.pallas_call(functools.partial(kernel, nz, ny, views, halfv, n_gz, n_xy...  141 us

profile of v3, /device:TPU:7, one launch (start us, length us, event | category | flops | bytes accessed | tf_op | source)
XLA Modules:
  0.0 143.1 jit_solution(2623760021732438160)
XLA Ops:
  0.0 141.1 %deconvolve.1 = f32[48,32,128]{2,1,0:T(8,128)} custom-call(s32[1,6]{1,0:T(1,128)} %bitcast.3, f32[6,61]{1,0:T(8,128)} %kd_ref.1, f32[6,31]{1,0:T(8,128)} %kr_ref.1, f32[6,31]{1,0:T(8,128)} %kc_ref.1, s32[3,128]{1,0:T(4,128)} %bitcast.2, f32[48,32,128]{2,1,0:T(8,128)} %est_hbm.1, f32[3,48,32,128]{3,2,1,0:T(8,128)} %up_hbm.1, f32[3,48,16,256]{3,2,1,0:T(8,128)} %vt_hbm.1), custom_call_target="tpu_custom_call" | custom-call | tf_op jit(solution)/shard_map/deconvolve/pallas_call | solution.py:524
  141.1 2.1 %copy.10 = f32[48,32,128]{2,1,0:T(8,128)} copy(f32[48,32,128]{2,1,0:T(8,128)} %deconvolve.1) | data formatting | bytes 1572864

commit v4 on v3

--- a/solution.py
+++ b/solution.py
@@ -180,7 +180,7 @@
     loads[1].wait()
     octets = nz // 8
 
-    @pl.loop(0, halfv * octets)
+    @pl.loop(0, halfv * octets, unroll=3)
     def _(i):
         block = vt[i // octets, pl.ds((i % octets) * 8, 8)].reshape(128, ny * n_xy)
         for half in range(2):
@@ -198,7 +198,7 @@
     for d in range(1, n_xy):
         turn(d).start()
 
-    @pl.loop(0, halfv * octets)
+    @pl.loop(0, halfv * octets, unroll=3)
     def _(i):
         recv[r, i] = pack[r, i]
 
@@ -211,7 +211,7 @@
             taps[n, 0:views, 64:64 + value.shape[1]] = value
     stack[...] = jnp.zeros_like(stack)
 
-    @pl.loop(0, views)
+    @pl.loop(0, views, unroll=2)
     def _(v):
         def toeplitz(line, count, shift):
             return pltpu.roll(jnp.broadcast_to(line, (count, 128)), shift, 1, stride=1, stride_axis=0)

time: 143 us -> 143 us (level)
  no operation moved by 1% of the time
where the time goes in v4:
time: 143 us
  Pallas kernels  141 us (99%)
  local copies, waits for them, and re-layouts  2.06 us (1%)
    pallas_call x1, Pallas kernels, local(): pl.pallas_call(functools.partial(kernel, nz, ny, views, halfv, n_gz, n_xy...  141 us

profile of v4, /device:TPU:7, one launch (start us, length us, event | category | flops | bytes accessed | tf_op | source)
XLA Modules:
  0.0 143.1 jit_solution(1787686918596157367)
XLA Ops:
  0.0 141.1 %deconvolve.1 = f32[48,32,128]{2,1,0:T(8,128)} custom-call(s32[1,6]{1,0:T(1,128)} %bitcast.3, f32[6,61]{1,0:T(8,128)} %kd_ref.1, f32[6,31]{1,0:T(8,128)} %kr_ref.1, f32[6,31]{1,0:T(8,128)} %kc_ref.1, s32[3,128]{1,0:T(4,128)} %bitcast.2, f32[48,32,128]{2,1,0:T(8,128)} %est_hbm.1, f32[3,48,32,128]{3,2,1,0:T(8,128)} %up_hbm.1, f32[3,48,16,256]{3,2,1,0:T(8,128)} %vt_hbm.1), custom_call_target="tpu_custom_call" | custom-call | tf_op jit(solution)/shard_map/deconvolve/pallas_call | solution.py:524
  141.1 2.1 %copy.10 = f32[48,32,128]{2,1,0:T(8,128)} copy(f32[48,32,128]{2,1,0:T(8,128)} %deconvolve.1) | data formatting | bytes 1572864
